TPU v7x, 128 devices: a whole 4x4x4 slice. The times are simulated.
128 devices in a mesh: attn: 4 (over z_hi, core), exp: 32 (over z_lo, y, x).
Axes of the slice: x: 4, y: 4, z: 4 (z_hi: 2, z_lo: 2; z = z_hi * 2 + z_lo), core: 2. Of those that a mesh axis runs over, the one named last changes fastest.
Arguments:
- tokens: bfloat16 [2, 1024, 7168], P(None, 'exp', 'attn'), may hold values from -6 to 6
- logits: float32 [2, 1024, 8], P(None, 'exp'), may hold values from -8 to 8
- routes: int32 [2, 1024, 8], P(None, 'exp'), may hold values from 0 to 31, all different within a row; in each aligned block of 32 rows (0 to 31, 32 to 63, ..., all dimensions but the last counted through in order) at most 16 rows name the same one
- held: int32 [32], replicated, may hold values from 0 to 31, each once
- swapped: int32 [16], replicated, may hold values 0 or 1
- w_gate: bfloat16 [32, 7168, 1024], P('exp', None, 'attn'), may hold values from -0.0625 to 0.0625
- w_up: bfloat16 [32, 7168, 1024], P('exp', None, 'attn'), may hold values from -0.0625 to 0.0625
- w_down: bfloat16 [32, 1024, 7168], P('exp', None, 'attn'), may hold values from -0.1875 to 0.1875
Outputs:
- mixed: bfloat16 [2, 1024, 7168], P(None, 'exp', 'attn')
- gate_after: bfloat16 [32, 7168, 1024], P('exp', None, 'attn')
- up_after: bfloat16 [32, 7168, 1024], P('exp', None, 'attn')
- down_after: bfloat16 [32, 1024, 7168], P('exp', None, 'attn')
Inputs may be any that keep to these rules, and one draw needn't show every extreme that they name: `routes`: each row names 8 different experts; in each step, no expert is named by more than 16 rows of one index of exp, and some expert by exactly that many in some of them. `held`: each expert id once.
All inputs are finite; a program needn't handle non-finite values.
Results may differ from a plain program's by a relative error of at most 0.0058.
Values may be sent and summed in bfloat16 or wider, within the bound.
A program may use at most 128 MiB of HBM per device.

v0:
```python
import jax
import jax.numpy as jnp
from jax import lax
from jax.sharding import PartitionSpec as P


def from_partner(value, axis, bit):
    mask = 2**bit
    pairs = [(source, source ^ mask) for source in range(lax.axis_size(axis))]
    return lax.ppermute(value, axis, pairs)


def slot_index(route_block, owner_of, capacity):
    flat = route_block.reshape(-1)
    experts_all = owner_of.shape[0]
    onehot = (flat[:, None] == jnp.arange(experts_all, dtype=jnp.int32)[None, :]).astype(jnp.int32)
    ranked = jnp.cumsum(onehot, axis=0)
    slots = jnp.sum(ranked * onehot, axis=1) - 1
    target = jnp.sum(onehot * owner_of[None, :], axis=1)
    return target * capacity + slots


def select_matrix(index, total):
    return (index[:, None] == jnp.arange(total, dtype=jnp.int32)[None, :]).astype(jnp.bfloat16)


def per_device(tokens, logits, routes, held, swapped, w_gate, w_up, w_down):
    exp_count = lax.axis_size("exp")
    own_index = lax.axis_index("exp")
    half_count = exp_count // 2
    others = from_partner((w_gate, w_up, w_down), "exp", exp_count.bit_length() - 2)
    own_flag = swapped[own_index % half_count]
    gate_after = jnp.where(own_flag == 1, others[0], w_gate)
    up_after = jnp.where(own_flag == 1, others[1], w_up)
    down_after = jnp.where(own_flag == 1, others[2], w_down)
    devices = jnp.arange(exp_count, dtype=jnp.int32)
    flags = swapped[devices % half_count]
    expert_after = jnp.where(flags == 1, held[jnp.bitwise_xor(devices, half_count)], held)
    gate_tile, up_tile, down_tile = (gate_after[0], up_after[0], down_after[0])
    expert_ids = jnp.arange(exp_count, dtype=jnp.int32)
    owner_of = jnp.sum(
        (expert_after[None, :] == expert_ids[:, None]).astype(jnp.int32) * devices[None, :], axis=1
    )
    rows_here = tokens.shape[1]
    top_count = routes.shape[2]
    quarter = tokens.shape[2]
    hidden_part = gate_tile.shape[1]
    capacity = min(rows_here, 2 * rows_here * top_count // exp_count)
    total = exp_count * capacity
    pieces = []
    for step in range(tokens.shape[0]):
        step_tokens = tokens[step : step + 1]
        step_logits = logits[step : step + 1]
        step_routes = routes[step : step + 1]
        step_count = step_tokens.shape[0]
        process_step = 0
        chooser = select_matrix(slot_index(step_routes[process_step], owner_of, capacity), total)
        selects = [chooser]
        placed = jnp.sum(chooser.reshape(rows_here, top_count, total), axis=1)
        buffer = jnp.einsum(
            "rm,rd->md", placed, step_tokens[process_step], preferred_element_type=jnp.float32
        )
        sends = [buffer.astype(jnp.bfloat16).reshape(exp_count, capacity, quarter)]
        outgoing = jnp.stack(sends, axis=1).reshape(exp_count, step_count * capacity, quarter)
        received = lax.all_to_all(outgoing, "exp", split_axis=0, concat_axis=0, tiled=True)
        items = received.shape[1]
        flat_rows = exp_count * items
        piece = lax.all_gather(received, "attn", axis=2, tiled=True)
        width = piece.shape[2]
        rows = piece.reshape(flat_rows, width)
        gate = jnp.dot(rows, gate_tile, preferred_element_type=jnp.float32)
        upper = jnp.dot(rows, up_tile, preferred_element_type=jnp.float32)
        hidden = (
            (jax.nn.silu(gate) * upper).astype(jnp.bfloat16).reshape(exp_count, items, hidden_part)
        )
        add_piece = lax.all_gather(hidden, "attn", axis=2, tiled=True)
        add_width = add_piece.shape[2]
        produced = jnp.dot(
            add_piece.reshape(flat_rows, add_width), down_tile, preferred_element_type=jnp.float32
        )
        served = produced.astype(jnp.bfloat16).reshape(exp_count, items, quarter)
        returned = lax.all_to_all(served, "exp", split_axis=0, concat_axis=0, tiled=True).reshape(
            exp_count, step_count, capacity, quarter
        )
        process_step = 0
        picked = jnp.dot(
            selects[process_step],
            returned[:, process_step].reshape(total, quarter),
            preferred_element_type=jnp.float32,
        )
        picked = picked.reshape(rows_here, top_count, quarter)
        score = jax.nn.sigmoid(step_logits[process_step])
        weight = score / jnp.sum(score, axis=-1, keepdims=True)
        results = [(2.5 * jnp.sum(weight[:, :, None] * picked, axis=1)).astype(jnp.bfloat16)]
        pieces.append(jnp.stack(results, axis=0))
    mixed = jnp.concatenate(pieces, axis=0)
    return (mixed, gate_after, up_after, down_after)


def solution(mesh):
    in_specs = (
        P(None, "exp", "attn"),
        P(None, "exp", None),
        P(None, "exp", None),
        P(),
        P(),
        P("exp", None, "attn"),
        P("exp", None, "attn"),
        P("exp", None, "attn"),
    )
    out_specs = (
        P(None, "exp", "attn"),
        P("exp", None, "attn"),
        P("exp", None, "attn"),
        P("exp", None, "attn"),
    )
    return jax.shard_map(
        per_device, mesh=mesh, in_specs=in_specs, out_specs=out_specs, check_vma=False
    )
```

profile of v0, /device:TPU:0, one launch (start us, length us, event | category | flops | bytes accessed | tf_op | source)
XLA Modules:
  0.0 501.1 jit_solution(13864764400353886560)
XLA Ops:
  7.2 0.7 fusion.48
  10.2 1.4 gather_fusion
  11.5 1.4 gather_fusion.1
  12.9 0.7 compare_select_fusion.2
  14.1 1.6 convolution_convert_fusion.1
  15.7 33.9 %all_to_all.20 = bf16[32,16,1792]{2,1,0:T(8,128)(2,1)} all-to-all(bf16[32,16,1792]{2,1,0:T(8,128)(2,1)S(1)} %bitcast.114), channel_id=1, replica_groups=mesh['attn'=4,'exp'=32] {'exp'}, dimensions={0} | all-to-all | bytes 3670016 | tf_op jit(solution)/shard_map/all_to_all | solution.py:65
  50.0 0.7 convolution_convert_fusion
  50.7 28.3 %all_to_all.21 = bf16[32,16,1792]{2,1,0:T(8,128)(2,1)} all-to-all(bf16[32,16,1792]{2,1,0:T(8,128)(2,1)S(1)} %bitcast.115), channel_id=1, replica_groups=mesh['attn'=4,'exp'=32] {'exp'}, dimensions={0} | all-to-all | bytes 3670016 | tf_op jit(solution)/shard_map/all_to_all | solution.py:65
  79.1 1.4 collective-permute-start
  80.5 0.7 collective-permute-start.1
  81.2 1.4 collective-permute-start.2
  83.8 137.1 %collective-permute-done = bf16[1,7168,256]{2,1,0:T(8,128)(2,1)} collective-permute-done((bf16[1,7168,256]{2,1,0:T(8,128)(2,1)}, bf16[1,7168,256]{2,1,0:T(8,128)(2,1)}, u32[]{:S(2)}, u32[]{:S(2)}) %collective-permute-start) | collective-permute-done | bytes 3670048 | tf_op jit(solution)/shard_map/ppermute | solution.py:10
  220.9 4.4 broadcast_select_fusion.2
  225.3 88.6 %collective-permute-done.1 = bf16[1,7168,256]{2,1,0:T(8,128)(2,1)} collective-permute-done((bf16[1,7168,256]{2,1,0:T(8,128)(2,1)}, bf16[1,7168,256]{2,1,0:T(8,128)(2,1)}, u32[]{:S(2)}, u32[]{:S(2)}) %collective-permute-start.1) | collective-permute-done | bytes 3670048 | tf_op jit(solution)/shard_map/ppermute | solution.py:10
  313.9 2.2 broadcast_select_fusion.1
  316.2 6.3 %fusion.10 = f32[512,256]{1,0:T(8,128)S(1)} fusion(bf16[512,7168]{1,0:T(8,128)(2,1)} %bitcast.123, bf16[1,7168,256]{2,1,0:T(8,128)(2,1)} %broadcast_select_fusion.2), kind=kOutput, calls=%fused_computation.12 | convolution fusion | flops 1879048192 | bytes 11534336 | tf_op jit(solution)/shard_map/dot_general | solution.py:71
  322.5 1.0 copy-done.7
  323.5 2.8 multiply_convert_fusion.1
  326.5 70.4 %collective-permute-done.2 = bf16[1,1024,1792]{2,1,0:T(8,128)(2,1)} collective-permute-done((bf16[1,1024,1792]{2,1,0:T(8,128)(2,1)}, bf16[1,1024,1792]{2,1,0:T(8,128)(2,1)}, u32[]{:S(2)}, u32[]{:S(2)}) %collective-permute-start.2) | collective-permute-done | bytes 3670048 | tf_op jit(solution)/shard_map/ppermute | solution.py:10
  396.9 4.3 broadcast_select_fusion
  401.1 6.3 %fusion.8 = f32[512,256]{1,0:T(8,128)S(1)} fusion(bf16[512,7168]{1,0:T(8,128)(2,1)} %bitcast.121, bf16[1,7168,256]{2,1,0:T(8,128)(2,1)} %broadcast_select_fusion.2), kind=kOutput, calls=%fused_computation.10 | convolution fusion | flops 1879048192 | bytes 11534336 | tf_op jit(solution)/shard_map/dot_general | solution.py:71
  407.5 1.0 copy-done.6
  408.5 2.8 multiply_convert_fusion
  411.3 5.7 %fusion.12 = bf16[512,1792]{1,0:T(8,128)(2,1)} fusion(bf16[512,1024]{1,0:T(8,128)(2,1)} %bitcast.125, bf16[1,1024,1792]{2,1,0:T(8,128)(2,1)} %broadcast_select_fusion), kind=kOutput, calls=%fused_computation.17 | convolution fusion | flops 1879965696 | bytes 6553600 | tf_op jit(solution)/shard_map/dot_general | solution.py:78
  417.0 6.2 %all-to-all-start.1 = ((bf16[32,16,1792]{2,1,0:T(8,128)(2,1)}), bf16[32,16,1792]{2,1,0:T(8,128)(2,1)S(1)}, u32[]{:S(2)}, u32[]{:S(2)}) async-start(bf16[32,16,1792]{2,1,0:T(8,128)(2,1)} %bitcast.118), calls=%async_computation.1 | async-start | bytes 3670016 | tf_op jit(solution)/shard_map/all_to_all | solution.py:82
  423.1 29.6 %all-gather.11.cloned.1.call-done = bf16[32,16,1024]{2,1,0:T(8,128)(2,1)} async-done(((bf16[32,16,256]{2,1,0:T(8,128)(2,1)}), bf16[32,16,1024]{2,1,0:T(8,128)(2,1)}) %all-gather.11.cloned.1.call-update) | async-done | bytes 1048592 | tf_op jit(solution)/shard_map/all_gather | solution.py:76
  452.8 5.7 %fusion.15 = bf16[512,1792]{1,0:T(8,128)(2,1)} fusion(bf16[512,1024]{1,0:T(8,128)(2,1)} %bitcast.126, bf16[1,1024,1792]{2,1,0:T(8,128)(2,1)} %broadcast_select_fusion), kind=kOutput, calls=%fused_computation.18 | convolution fusion | flops 1879965696 | bytes 6553600 | tf_op jit(solution)/shard_map/dot_general | solution.py:78
  458.4 7.4 %all-to-all-start.3 = ((bf16[32,16,1792]{2,1,0:T(8,128)(2,1)}), bf16[32,16,1792]{2,1,0:T(8,128)(2,1)}, u32[]{:S(2)}, u32[]{:S(2)}) async-start(bf16[32,16,1792]{2,1,0:T(8,128)(2,1)} %bitcast.117), calls=%async_computation.3 | async-start | bytes 3670016 | tf_op jit(solution)/shard_map/all_to_all | solution.py:82
  466.1 0.8 fusion.18
  466.9 24.6 %all-to-all-done.3 = bf16[32,16,1792]{2,1,0:T(8,128)(2,1)} async-done(((bf16[32,16,1792]{2,1,0:T(8,128)(2,1)}), bf16[32,16,1792]{2,1,0:T(8,128)(2,1)}, u32[]{:S(2)}, u32[]{:S(2)}) %all-to-all-start.3) | async-done | bytes 1835040 | tf_op jit(solution)/shard_map/all_to_all | solution.py:82
  491.6 2.3 fusion.19
  493.9 0.7 pad_maximum_fusion
  (60 shorter events, 4.3 us)
Async XLA Ops:
  7.2 309.0 %all-gather.5.cloned.1.call-start = ((), (), s32[]{:S(2)}) async-start(), calls=%async_computation.4 | async-start | bytes 9175040 | tf_op jit(solution)/shard_map/all_gather | solution.py:68
  14.1 35.9 %copy-start.4 = (bf16[2,32,1792]{2,1,0:T(8,128)(2,1)S(1)}, bf16[2,32,1792]{2,1,0:T(8,128)(2,1)}, u32[]{:S(2)}) copy-start(bf16[2,32,1792]{2,1,0:T(8,128)(2,1)} %param.8) | copy-start | bytes 688132
  49.6 351.5 %all-gather.9.cloned.1.call-start = ((), (), s32[]{:S(2)}) async-start(), calls=%async_computation.6 | async-start | bytes 9175040 | tf_op jit(solution)/shard_map/all_gather | solution.py:68
  50.0 32.5 %copy-start = (s32[16]{0:T(128)S(1)}, s32[16]{0:T(128)}, u32[]{:S(2)}) copy-start(s32[16]{0:T(128)} %param.12) | copy-start | bytes 196
  79.0 332.3 %all-gather.7.cloned.1.call-start = ((), (), s32[]{:S(2)}) async-start(), calls=%async_computation.5 | async-start | bytes 1310720 | tf_op jit(solution)/shard_map/all_gather | solution.py:76
  79.1 141.8 %collective-permute-start = (bf16[1,7168,256]{2,1,0:T(8,128)(2,1)}, bf16[1,7168,256]{2,1,0:T(8,128)(2,1)}, u32[]{:S(2)}, u32[]{:S(2)}) collective-permute-start(bf16[1,7168,256]{2,1,0:T(8,128)(2,1)} %param.13), channel_id=1, source_target_pairs={{0,16},{1,17},{2,18},{3,19},{4,20},{5,21},{6,22},{7,23},{8,24},{9,... | collective-permute-start | bytes 11010056 | tf_op jit(solution)/shard_map/ppermute | solution.py:10
  80.5 233.4 %collective-permute-start.1 = (bf16[1,7168,256]{2,1,0:T(8,128)(2,1)}, bf16[1,7168,256]{2,1,0:T(8,128)(2,1)}, u32[]{:S(2)}, u32[]{:S(2)}) collective-permute-start(bf16[1,7168,256]{2,1,0:T(8,128)(2,1)} %param.14), channel_id=1, source_target_pairs={{0,16},{1,17},{2,18},{3,19},{4,20},{5,21},{6,22},{7,23},{8,24},{9,... | collective-permute-start | bytes 11010056 | tf_op jit(solution)/shard_map/ppermute | solution.py:10
  81.2 315.7 %collective-permute-start.2 = (bf16[1,1024,1792]{2,1,0:T(8,128)(2,1)}, bf16[1,1024,1792]{2,1,0:T(8,128)(2,1)}, u32[]{:S(2)}, u32[]{:S(2)}) collective-permute-start(bf16[1,1024,1792]{2,1,0:T(8,128)(2,1)} %param.15), channel_id=1, source_target_pairs={{0,16},{1,17},{2,18},{3,19},{4,20},{5,21},{6,22},{7,23},{8,24},{9,... | collective-permute-start | bytes 11010056 | tf_op jit(solution)/shard_map/ppermute | solution.py:10
  220.9 93.1 %copy-start.1 = (bf16[1,7168,256]{2,1,0:T(8,128)(2,1)S(1)}, bf16[1,7168,256]{2,1,0:T(8,128)(2,1)}, u32[]{:S(2)}) copy-start(bf16[1,7168,256]{2,1,0:T(8,128)(2,1)} %param.14) | copy-start | bytes 11010052
  316.2 6.3 %copy-start.2 = (bf16[1,7168,256]{2,1,0:T(8,128)(2,1)S(1)}, bf16[1,7168,256]{2,1,0:T(8,128)(2,1)}, u32[]{:S(2)}) copy-start(bf16[1,7168,256]{2,1,0:T(8,128)(2,1)} %broadcast_select_fusion.1) | copy-start | bytes 11010052
  316.2 7.3 %copy-start.7 = (bf16[32,16,7168]{2,1,0:T(8,128)(2,1)S(1)}, bf16[32,16,7168]{2,1,0:T(8,128)(2,1)}, u32[]{:S(2)}) copy-start(bf16[32,16,7168]{2,1,0:T(8,128)(2,1)} %all-gather.5.cloned.1.call-done) | copy-start | bytes 22020100
  326.3 126.5 %all-gather.11.cloned.1.call-start = ((), (), s32[]{:S(2)}) async-start(), calls=%async_computation.7 | async-start | bytes 1310720 | tf_op jit(solution)/shard_map/all_gather | solution.py:76
  401.1 6.3 %copy-start.3 = (bf16[1,7168,256]{2,1,0:T(8,128)(2,1)S(1)}, bf16[1,7168,256]{2,1,0:T(8,128)(2,1)}, u32[]{:S(2)}) copy-start(bf16[1,7168,256]{2,1,0:T(8,128)(2,1)} %broadcast_select_fusion.1) | copy-start | bytes 11010052
  401.1 7.3 %copy-start.6 = (bf16[32,16,7168]{2,1,0:T(8,128)(2,1)S(1)}, bf16[32,16,7168]{2,1,0:T(8,128)(2,1)}, u32[]{:S(2)}) copy-start(bf16[32,16,7168]{2,1,0:T(8,128)(2,1)} %all-gather.9.cloned.1.call-done) | copy-start | bytes 22020100
  417.0 41.5 %all-to-all-start.1 = ((bf16[32,16,1792]{2,1,0:T(8,128)(2,1)}), bf16[32,16,1792]{2,1,0:T(8,128)(2,1)S(1)}, u32[]{:S(2)}, u32[]{:S(2)}) async-start(bf16[32,16,1792]{2,1,0:T(8,128)(2,1)} %bitcast.118), calls=%async_computation.1 | async-start | bytes 3670016 | tf_op jit(solution)/shard_map/all_to_all | solution.py:82
  458.4 7.4 %copy-start.5 = (f32[2,32,8]{1,2,0:T(8,128)S(1)}, f32[2,32,8]{1,2,0:T(8,128)}, u32[]{:S(2)}) copy-start(f32[2,32,8]{1,2,0:T(8,128)} %param.9) | copy-start | bytes 6148
  458.4 33.1 %all-to-all-start.3 = ((bf16[32,16,1792]{2,1,0:T(8,128)(2,1)}), bf16[32,16,1792]{2,1,0:T(8,128)(2,1)}, u32[]{:S(2)}, u32[]{:S(2)}) async-start(bf16[32,16,1792]{2,1,0:T(8,128)(2,1)} %bitcast.117), calls=%async_computation.3 | async-start | bytes 3670016 | tf_op jit(solution)/shard_map/all_to_all | solution.py:82
Sparse Core Ops, SparseCore 0:
  49.7 104.6 all-gather.4
  156.1 96.8 all-gather.8
  326.4 29.5 all-gather.6
  411.4 41.3 all-gather.10
where the time goes:
time: 502 us; the launch traced here: 501 us
  waiting for transfers between devices  350 us (70%)
  blocking collectives  62.2 us (12%)
  matrix products  34.9 us (7%)
  starting transfers between devices  17.4 us (3%)
  between operations  14.7 us (3%)
  other arithmetic  14.3 us (3%)
  local copies, waits for them, and re-layouts  7.19 us (1%)
    ppermute x3, waiting for transfers between devices, from_partner(): return lax.ppermute(value, axis, pairs)  296 us
    all_to_all x2, blocking collectives, per_device(): lax.all_to_all(outgoing, 'exp', split_axis=0, concat_axis=0, tiled=True)  62.2 us
    all_gather x2, waiting for transfers between devices, per_device(): add_piece = lax.all_gather(hidden, 'attn', axis=2, tiled=True)  29.7 us
    all_to_all x2, waiting for transfers between devices, per_device(): lax.all_to_all(served, 'exp', split_axis=0, concat_axis=0, tiled=True)  24.7 us
    all_to_all x2, starting transfers between devices, per_device(): lax.all_to_all(served, 'exp', split_axis=0, concat_axis=0, tiled=True)  13.6 us
    dot_general x2, matrix products, per_device(): gate = jnp.dot(rows, gate_tile, preferred_element_type=jnp.float32)  12.7 us
    dot_general x2, matrix products, per_device(): jnp.dot(add_piece.reshape(flat_rows, add_width), down_tile, preferred_ele...  11.3 us
  transfers between devices with their start and end apart: 9, of which 5 were waited for; matrix products, arithmetic and copies ran while one was open for 9% of the time, Pallas kernels for 0%

commit v1 on v0

v1 whole, which is shorter than its diff:
```python
import jax
import jax.numpy as jnp
from jax import lax
from jax.experimental import pallas as pl
from jax.experimental.pallas import tpu as pltpu
from jax.sharding import PartitionSpec as P

RING = 4


def wrap(value):
    return lax.rem(value + RING, RING)


def place():
    attn = lax.axis_index("attn")
    exp = lax.axis_index("exp")
    z_hi, core = attn // 2, lax.rem(attn, 2)
    z_lo, y, x = exp // 16, lax.rem(exp // 4, 4), lax.rem(exp, 4)
    return z_hi, core, z_lo, y, x


def device(z_hi, core, z_lo, y, x):
    return {"attn": z_hi * 2 + core, "exp": z_lo * 16 + y * 4 + x}


def neighbours(z_hi, core, z_lo, y, x):
    z = z_hi * 2 + z_lo
    right_z, left_z = wrap(z + 1), wrap(z - 1)
    along_z = [device(n // 2, core, lax.rem(n, 2), y, x) for n in (right_z, left_z)]
    along_x = [device(z_hi, core, z_lo, y, n) for n in (wrap(x + 1), wrap(x - 1))]
    along_y = [device(z_hi, core, z_lo, n, x) for n in (wrap(y + 1), wrap(y - 1))]
    return along_z, along_x, along_y, device(z_hi, 1 - core, z_lo, y, x)


def greet(devices):
    barrier = pltpu.get_barrier_semaphore()
    for other in devices:
        pl.semaphore_signal(barrier, inc=1, device_id=other, device_id_type=pl.DeviceIdType.MESH)
    pl.semaphore_wait(barrier, len(devices))


class Sends:
    def __init__(self, send_sem, recv_sem):
        self.send_sem, self.recv_sem, self.copies = send_sem, recv_sem, []

    def __call__(self, src, dst, to):
        k = len(self.copies)
        copy = pltpu.make_async_remote_copy(
            src_ref=src,
            dst_ref=dst,
            send_sem=self.send_sem.at[k],
            recv_sem=self.recv_sem.at[k],
            device_id=to,
            device_id_type=pl.DeviceIdType.MESH,
        )
        copy.start()
        self.copies.append(copy)
        return copy


GATHER_COPIES = 6 + 12 + 12 + 16


def gather_kernel(tok_ref, all_ref, local_sem, send_sem, recv_sem):
    z_hi, core, z_lo, y, x = place()
    along_z, along_x, along_y, sibling = neighbours(z_hi, core, z_lo, y, x)
    greet(along_z + along_x + along_y + [sibling])
    z = z_hi * 2 + z_lo
    quarter = tok_ref.shape[2]
    send = Sends(send_sem, recv_sem)

    def cols(high):
        return pl.ds(pl.multiple_of((high * 2 + core) * quarter, 128), quarter)

    def spot(step, at):
        return all_ref.at[step, lax.rem(at, 2), y, x, :, cols(at // 2)]

    own = [pltpu.make_async_copy(tok_ref.at[s], spot(s, z), local_sem.at[s]) for s in range(2)]
    for copy in own:
        copy.start()
    first = {}
    for s in range(2):
        for d in range(2):
            first[d, s] = send(tok_ref.at[s], spot(s, z), along_z[d])
    first[0, 0].wait_recv()
    forward0 = send(spot(0, wrap(z - 1)), spot(0, wrap(z - 1)), along_z[0])
    first[1, 1].wait_recv()
    forward1 = send(spot(1, wrap(z + 1)), spot(1, wrap(z + 1)), along_z[1])
    rest = {0: [first[1, 0], forward0], 1: [first[0, 1], forward1]}

    def line(step, axis, at, high):
        if axis == "x":
            return all_ref.at[step, :, y, at, :, cols(high)]
        return all_ref.at[step, :, at, x, :, cols(high)]

    def sheet(step, axis, at, high):
        if axis == "x":
            return all_ref.at[step, :, :, at, :, cols(high)]
        return all_ref.at[step, :, at, :, :, cols(high)]

    along = {"x": along_x, "y": along_y}
    spot_on = {"x": x, "y": y}
    order = (("x", "y"), ("y", "x"))

    def start_ring(unit, step, axis):
        return {
            (d, high): send(unit(step, axis, spot_on[axis], high), unit(step, axis, spot_on[axis], high), along[axis][d])
            for high in range(2)
            for d in range(2)
        }

    def forward_ring(copies, unit, step, axis):
        at = spot_on[axis]
        out = []
        for d in range(2):
            origin = wrap(at - 1) if d == 0 else wrap(at + 1)
            copies[d, d].wait_recv()
            out.append(send(unit(step, axis, origin, d), unit(step, axis, origin, d), along[axis][d]))
        return out

    lines, line_forwards = {}, {}
    for s in range(2):
        for copy in rest[s]:
            copy.wait_recv()
        own[s].wait()
        lines[s] = start_ring(line, s, order[s][0])
    for s in range(2):
        line_forwards[s] = forward_ring(lines[s], line, s, order[s][0])
    sheets, sheet_forwards, shared = {}, {}, []
    for s in range(2):
        lines[s][0, 1].wait_recv()
        lines[s][1, 0].wait_recv()
        for copy in line_forwards[s]:
            copy.wait_recv()
        sheets[s] = start_ring(sheet, s, order[s][1])

    def share(step, offset, high):
        axis = order[step][1]
        part = sheet(step, axis, wrap(spot_on[axis] + offset), high)
        shared.append(send(part, part, sibling))

    for s in range(2):
        for high in range(2):
            share(s, 0, high)
    for s in range(2):
        sheet_forwards[s] = forward_ring(sheets[s], sheet, s, order[s][1])
        share(s, -1, 0)
        share(s, 1, 1)
    for s in range(2):
        sheets[s][0, 1].wait_recv()
        share(s, -1, 1)
        sheets[s][1, 0].wait_recv()
        share(s, 1, 0)
    for s in range(2):
        for d in range(2):
            sheet_forwards[s][d].wait_recv()
            share(s, 2, d)
    for copy in shared:
        copy.wait_recv()
    for copy in send.copies:
        copy.wait_send()


def gather_tokens(tokens):
    steps, rows, quarter = tokens.shape
    out = pl.pallas_call(
        gather_kernel,
        out_shape=jax.ShapeDtypeStruct((steps, 2, RING, RING, rows, 4 * quarter), tokens.dtype),
        in_specs=[pl.BlockSpec(memory_space=pl.ANY)],
        out_specs=pl.BlockSpec(memory_space=pl.ANY),
        scratch_shapes=[
            pltpu.SemaphoreType.DMA((2,)),
            pltpu.SemaphoreType.DMA((GATHER_COPIES,)),
            pltpu.SemaphoreType.DMA((GATHER_COPIES,)),
        ],
        compiler_params=pltpu.CompilerParams(collective_id=0, has_side_effects=True),
        name="gather_tokens",
    )(tokens)
    return out.reshape(steps * 2 * RING * RING * rows, 4 * quarter)


REDUCE_COPIES = 2 * (2 + 4 + 2 + 2) + 2


def reduce_kernel(c_ref, out_ref, hop0, got0, sum0, hop1, got1, sum1, last, send_sem, recv_sem):
    z_hi, core, z_lo, y, x = place()
    along_z, along_x, along_y, _ = neighbours(z_hi, core, z_lo, y, x)
    partner = device(z_hi, core, 1 - z_lo, y, x)
    greet(along_x + along_y + [partner])
    along = {"x": along_x, "y": along_y}
    spot_on = {"x": x, "y": y}
    order = (("y", "x"), ("x", "y"))
    send = Sends(send_sem, recv_sem)

    def block(step, at):
        if order[step][0] == "y":
            return c_ref.at[step, :, at]
        return c_ref.at[step, :, :, at]

    hops, fulls = {}, {}
    for s in range(2):
        axis = order[s][0]
        at = spot_on[axis]
        hops[s] = [send(block(s, wrap(at + 2)).at[d], hop0.at[s, d], along[axis][d]) for d in range(2)]
    for s in range(2):
        axis = order[s][0]
        at = spot_on[axis]
        for d in range(2):
            target = wrap(at + 1) if d == 0 else wrap(at - 1)
            fulls[s, d] = [send(block(s, target).at[1 - d], got0.at[s, d, 1 - d], along[axis][d])]
    for s in range(2):
        axis = order[s][0]
        at = spot_on[axis]
        for d in range(2):
            target = wrap(at + 1) if d == 0 else wrap(at - 1)
            hops[s][d].wait_recv()
            mine = block(s, target)

            @pl.loop(0, RING)
            def _(i, mine=mine, s=s, d=d):
                total = mine[d, i].astype(jnp.float32) + hop0[s, d, i].astype(jnp.float32)
                hop0[s, d, i] = total.astype(jnp.bfloat16)

            fulls[s, d].append(send(hop0.at[s, d], got0.at[s, d, d], along[axis][d]))
    hops1, fulls1 = {}, {}
    for s in range(2):
        at = spot_on[order[s][0]]
        mine = block(s, at)
        for d in range(2):
            for copy in fulls[s, d]:
                copy.wait_recv()

        @pl.loop(0, RING)
        def _(i, mine=mine, s=s):
            for half in range(2):
                total = mine[half, i].astype(jnp.float32)
                total = total + got0[s, 0, half, i].astype(jnp.float32)
                total = total + got0[s, 1, half, i].astype(jnp.float32)
                sum0[s, half, i] = total.astype(jnp.bfloat16)

        axis = order[s][1]
        at = spot_on[axis]
        hops1[s] = [send(sum0.at[s, d, wrap(at + 2)], hop1.at[s, d], along[axis][d]) for d in range(2)]
    for s in range(2):
        axis = order[s][1]
        at = spot_on[axis]
        for d in range(2):
            target = wrap(at + 1) if d == 0 else wrap(at - 1)
            hops1[s][d].wait_recv()
            total = sum0[s, d, target].astype(jnp.float32) + hop1[s, d].astype(jnp.float32)
            sum0[s, d, target] = total.astype(jnp.bfloat16)
            fulls1[s, d] = send(sum0.at[s, :, target], got1.at[s, d], along[axis][d])
    finals = []
    for s in range(2):
        at = spot_on[order[s][1]]
        for d in range(2):
            fulls1[s, d].wait_recv()
        for half in range(2):
            total = sum0[s, half, at].astype(jnp.float32)
            total = total + got1[s, 0, half].astype(jnp.float32)
            total = total + got1[s, 1, half].astype(jnp.float32)
            sum1[s, half] = total.astype(jnp.bfloat16)
        finals.append(send(sum1.at[s, 1 - z_lo], last.at[s], partner))
    for s in range(2):
        finals[s].wait_recv()
        total = sum1[s, z_lo].astype(jnp.float32) + last[s].astype(jnp.float32)
        out_ref[s] = total.astype(jnp.bfloat16)
    for copy in send.copies:
        copy.wait_send()


def reduce_outputs(parts):
    steps, _, _, _, rows, width = parts.shape
    dt = parts.dtype
    return pl.pallas_call(
        reduce_kernel,
        out_shape=jax.ShapeDtypeStruct((steps, rows, width), dt),
        in_specs=[pl.BlockSpec(memory_space=pltpu.VMEM)],
        out_specs=pl.BlockSpec(memory_space=pltpu.VMEM),
        scratch_shapes=[
            pltpu.VMEM((steps, 2, RING, rows, width), dt),
            pltpu.VMEM((steps, 2, 2, RING, rows, width), dt),
            pltpu.VMEM((steps, 2, RING, rows, width), dt),
            pltpu.VMEM((steps, 2, rows, width), dt),
            pltpu.VMEM((steps, 2, 2, rows, width), dt),
            pltpu.VMEM((steps, 2, rows, width), dt),
            pltpu.VMEM((steps, rows, width), dt),
            pltpu.SemaphoreType.DMA((REDUCE_COPIES,)),
            pltpu.SemaphoreType.DMA((REDUCE_COPIES,)),
        ],
        compiler_params=pltpu.CompilerParams(
            collective_id=1, has_side_effects=True, vmem_limit_bytes=40 * 1024 * 1024
        ),
        name="reduce_outputs",
    )(parts)


def from_partner(value, axis, bit):
    mask = 2**bit
    pairs = [(source, source ^ mask) for source in range(lax.axis_size(axis))]
    return lax.ppermute(value, axis, pairs)


def per_device(tokens, logits, routes, held, swapped, w_gate, w_up, w_down):
    exp_count = lax.axis_size("exp")
    own_index = lax.axis_index("exp")
    half_count = exp_count // 2
    steps, rows_here, quarter = tokens.shape
    others = [from_partner(w, "exp", exp_count.bit_length() - 2) for w in (w_gate, w_up, w_down)]
    own_flag = swapped[own_index % half_count]

    score = jax.nn.sigmoid(logits)
    weight = score / jnp.sum(score, axis=-1, keepdims=True)
    expert_ids = jnp.arange(exp_count, dtype=jnp.int32)
    named = routes[:, :, :, None] == expert_ids
    table = jnp.sum(jnp.where(named, weight[:, :, :, None], 0.0), axis=2)
    everyone = lax.all_gather(table, "exp", axis=1, tiled=True)
    own_expert = held[own_index]
    own_weight = jnp.sum(jnp.where(expert_ids == own_expert, everyone, 0.0), axis=2)

    rows = gather_tokens(tokens)
    gate_tile, up_tile, down_tile = w_gate[0], w_up[0], w_down[0]
    gate = jnp.dot(rows, gate_tile, preferred_element_type=jnp.float32)
    upper = jnp.dot(rows, up_tile, preferred_element_type=jnp.float32)
    hidden = (jax.nn.silu(gate) * upper).astype(jnp.bfloat16)
    hidden = lax.all_gather(hidden, "attn", axis=1, tiled=True)
    produced = jnp.dot(hidden, down_tile, preferred_element_type=jnp.float32).astype(jnp.bfloat16)
    scaled = (2.5 * own_weight.reshape(-1)[:, None] * produced.astype(jnp.float32)).astype(jnp.bfloat16)
    mixed = reduce_outputs(scaled.reshape(steps, 2, RING, RING, rows_here, quarter))

    own_flag, mixed = lax.optimization_barrier((own_flag, mixed))
    afters = [jnp.where(own_flag == 1, other, w) for other, w in zip(others, (w_gate, w_up, w_down))]
    return (mixed, *afters)


def solution(mesh):
    in_specs = (
        P(None, "exp", "attn"),
        P(None, "exp", None),
        P(None, "exp", None),
        P(),
        P(),
        P("exp", None, "attn"),
        P("exp", None, "attn"),
        P("exp", None, "attn"),
    )
    out_specs = (
        P(None, "exp", "attn"),
        P("exp", None, "attn"),
        P("exp", None, "attn"),
        P("exp", None, "attn"),
    )
    return jax.shard_map(
        per_device, mesh=mesh, in_specs=in_specs, out_specs=out_specs, check_vma=False
    )
```

time: 502 us -> 433 us (0.86)
  waiting for transfers between devices: 350 us -> 0.03 us
  Pallas kernels: 0 us -> 275 us
  blocking collectives: 62.2 us -> 85.7 us
  starting transfers between devices: 17.4 us -> 3.64 us
  matrix products: 34.9 us -> 40 us
    ppermute x3, waiting for transfers between devices: 296 us -> 0.01 us  [from_partner(): return lax.ppermute(value, axis, pairs)]
    pallas_call x0 -> x2, Pallas kernels: none -> 275 us  [the longest x1 176 us: reduce_outputs(): pl.pallas_call(reduce_kernel, out_shape=jax.ShapeDtypeStruct((steps, rows...]
    all_gather x0 -> x1, blocking collectives: none -> 85.7 us  [per_device(): everyone = lax.all_gather(table, 'exp', axis=1, tiled=True)]
    all_to_all x2 -> x0, blocking collectives: 62.2 us -> none  [per_device(): lax.all_to_all(outgoing, 'exp', split_axis=0, concat_axis=0, tiled=True)]
    all_gather x4 -> x1, waiting for transfers between devices: 29.7 us -> 0.01 us  [per_device(): hidden = lax.all_gather(hidden, 'attn', axis=1, tiled=True)]
    all_to_all x2 -> x0, waiting for transfers between devices: 24.7 us -> none  [per_device(): lax.all_to_all(served, 'exp', split_axis=0, concat_axis=0, tiled=True)]
    all_to_all x2 -> x0, starting transfers between devices: 13.6 us -> none  [per_device(): lax.all_to_all(served, 'exp', split_axis=0, concat_axis=0, tiled=True)]
    dot_general x2 -> x1, matrix products: 5.53 us -> 14.9 us  [per_device(): upper = jnp.dot(rows, up_tile, preferred_element_type=jnp.float32)]
  transfers between devices with their start and end apart: 9 -> 4, of which waited for: 5 -> 0; matrix products, arithmetic and copies ran while one was open for 9% -> 5% of each run, Pallas kernels for 0% -> 41%
where the time goes in v1:
time: 433 us; the launch traced here: 432 us
  Pallas kernels  275 us (64%)
  blocking collectives  85.7 us (20%)
  matrix products  40 us (9%)
  between operations  14.9 us (3%)
  other arithmetic  10.1 us (2%)
    pallas_call x1, Pallas kernels, reduce_outputs(): pl.pallas_call(reduce_kernel, out_shape=jax.ShapeDtypeStruct((steps, rows...  176 us
    pallas_call x1, Pallas kernels, gather_tokens(): pl.pallas_call(gather_kernel, out_shape=jax.ShapeDtypeStruct((steps, 2, R...  99.2 us
    all_gather x1, blocking collectives, per_device(): everyone = lax.all_gather(table, 'exp', axis=1, tiled=True)  85.7 us
    dot_general x1, matrix products, per_device(): upper = jnp.dot(rows, up_tile, preferred_element_type=jnp.float32)  14.9 us
    dot_general x1, matrix products, per_device(): gate = jnp.dot(rows, gate_tile, preferred_element_type=jnp.float32)  14.5 us
    dot_general x1, matrix products, per_device(): jnp.dot(hidden, down_tile, preferred_element_type=jnp.float32)  10.6 us
    select_n x3, other arithmetic, per_device(): jnp.where(own_flag == 1, other, w)  8.9 us
  transfers between devices with their start and end apart: 4, of which 0 were waited for; matrix products, arithmetic and copies ran while one was open for 5% of the time, Pallas kernels for 41%

profile of v1, /device:TPU:0, one launch (start us, length us, event | category | flops | bytes accessed | tf_op | source)
XLA Modules:
  0.0 432.5 jit_solution(3978520316697456138)
XLA Ops:
  7.2 0.0 all-gather.2.cloned.1.call-start
  7.2 99.2 %gather_tokens.1 = bf16[2,2,4,4,32,7168]{5,4,3,2,1,0:T(8,128)(2,1)} custom-call(bf16[2,32,1792]{2,1,0:T(8,128)(2,1)} %tok_ref.1), custom_call_target="tpu_custom_call" | custom-call | tf_op jit(solution)/shard_map/gather_tokens/pallas_call | solution.py:167
  106.4 0.0 copy-start
  106.4 14.5 %fusion.3 = f32[2048,256]{1,0:T(8,128)S(1)} fusion(bf16[2048,7168]{1,0:T(8,128)(2,1)} %bitcast.26, bf16[1,7168,256]{2,1,0:T(8,128)(2,1)} %param.13), kind=kOutput, calls=%fused_computation.5 | convolution fusion | flops 7516192768 | bytes 35127296 | tf_op jit(solution)/shard_map/dot_general | solution.py:324
  121.0 0.0 copy-start.3
  121.0 0.0 copy-start.4
  121.0 0.0 copy-start.5
  121.0 0.0 copy-start.6
  121.0 14.9 %fusion.8 = bf16[2048,256]{1,0:T(8,128)(2,1)} fusion(bf16[2048,7168]{1,0:T(8,128)(2,1)} %bitcast.27, bf16[1,7168,256]{2,1,0:T(8,128)(2,1)S(1)} %copy-done, f32[2048,256]{1,0:T(8,128)S(1)} %fusion.3), kind=kOutput, calls=%fused_computation.11 | convolution fusion | flops 7519338496 | bytes 36175872 | tf_op jit(solution)/shard_map/dot_general | solution.py:325
  135.9 0.0 all-gather.2.cloned.1.call-update
  135.9 1.6 collective-permute-start.2
  137.5 0.5 collective-permute-start.1
  138.0 1.5 collective-permute-start
  139.6 0.1 copy.15
  139.7 0.1 copy.14
  139.8 0.6 dynamic_slice.7
  140.4 0.6 iota_compare_fusion.1
  141.0 0.2 select_reduce_fusion.1
  141.2 85.7 %all_gather.6 = f32[2,1024,32]{2,1,0:T(8,128)S(1)} all-gather(f32[2,32,32]{2,1,0:T(8,128)S(1)} %select_reduce_fusion.1), channel_id=1, replica_groups=mesh['attn'=4,'exp'=32] {'exp'}, dimensions={1}, use_global_device_ids=true | all-gather | bytes 270336 | tf_op jit(solution)/shard_map/all_gather | solution.py:318
  226.9 0.3 select_reduce_fusion
  227.3 0.6 dynamic_slice.6
  227.9 10.6 %multiply_convert_fusion = bf16[2048,1792]{1,0:T(8,128)(2,1)S(1)} fusion(f32[2048]{0:T(1024)S(1)} %bitcast.28, bf16[2048,1024]{1,0:T(8,128)(2,1)} %all-gather.2.cloned.1.call-done, bf16[1,1024,1792]{2,1,0:T(8,128)(2,1)} %param.15), kind=kOutput, calls=%fused_computation | convolution fusion | flops 7530872832 | bytes 15212544 | tf_op jit(solution)/shard_map/dot_general | solution.py:328
  238.5 175.7 %reduce_outputs.1 = bf16[2,32,1792]{2,1,0:T(8,128)(2,1)S(1)} custom-call(bf16[2,2,4,4,32,1792]{5,4,3,2,1,0:T(8,128)(2,1)S(1)} %bitcast.25), custom_call_target="tpu_custom_call" | custom-call | tf_op jit(solution)/shard_map/reduce_outputs/pallas_call | solution.py:276
  414.9 0.0 copy-start.1
  414.9 0.0 collective-permute-done.2
  415.0 4.4 %broadcast_select_fusion = bf16[1,1024,1792]{2,1,0:T(8,128)(2,1)} fusion(bf16[1,1024,1792]{2,1,0:T(8,128)(2,1)} %collective-permute-done.2, bf16[1,1024,1792]{2,1,0:T(8,128)(2,1)} %param.15, pred[]{:T(512)S(6)} %eq.31), kind=kLoop, calls=%fused_computation.7 | loop fusion | flops 1835008 | bytes 11010049 | tf_op jit(solution)/shard_map/jit(_where)/select_n | solution.py:333
  419.4 0.0 collective-permute-done.1
  419.4 2.3 broadcast_select_fusion.1
  421.6 0.0 collective-permute-done
  421.6 1.1 copy-done.2
  422.7 2.2 broadcast_select_fusion.2
  425.0 0.7 copy.22
  (12 shorter events, 0.1 us)
Async XLA Ops:
  7.2 220.7 %all-gather.2.cloned.1.call-start = ((), (), s32[]{:S(2)}) async-start(), calls=%async_computation | async-start | bytes 5242880 | tf_op jit(solution)/shard_map/all_gather | solution.py:327
  106.4 14.5 %copy-start = (bf16[1,7168,256]{2,1,0:T(8,128)(2,1)S(1)}, bf16[1,7168,256]{2,1,0:T(8,128)(2,1)}, u32[]{:S(2)}) copy-start(bf16[1,7168,256]{2,1,0:T(8,128)(2,1)} %param.14) | copy-start | bytes 11010052
  121.0 18.6 %copy-start.3 = (f32[2,32,8]{1,2,0:T(8,128)S(1)}, f32[2,32,8]{1,2,0:T(8,128)}, u32[]{:S(2)}) copy-start(f32[2,32,8]{1,2,0:T(8,128)} %param.9) | copy-start | bytes 6148
  121.0 18.7 %copy-start.4 = (s32[2,32,8]{1,2,0:T(8,128)S(1)}, s32[2,32,8]{1,2,0:T(8,128)}, u32[]{:S(2)}) copy-start(s32[2,32,8]{1,2,0:T(8,128)} %param.10) | copy-start | bytes 6148
  121.0 18.8 %copy-start.5 = (s32[32]{0:T(128)S(1)}, s32[32]{0:T(128)}, u32[]{:S(2)}) copy-start(s32[32]{0:T(128)} %param.11) | copy-start | bytes 388
  121.0 106.3 %copy-start.6 = (s32[16]{0:T(128)S(1)}, s32[16]{0:T(128)}, u32[]{:S(2)}) copy-start(s32[16]{0:T(128)} %param.12) | copy-start | bytes 196
  135.9 279.0 %collective-permute-start.2 = (bf16[1,1024,1792]{2,1,0:T(8,128)(2,1)}, bf16[1,1024,1792]{2,1,0:T(8,128)(2,1)}, u32[]{:S(2)}, u32[]{:S(2)}) collective-permute-start(bf16[1,1024,1792]{2,1,0:T(8,128)(2,1)} %param.15), channel_id=1, source_target_pairs={{0,16},{1,17},{2,18},{3,19},{4,20},{5,21},{6,22},{7,23},{8,24},{9,... | collective-permute-start | bytes 11010056 | tf_op jit(solution)/shard_map/ppermute | solution.py:302
  137.5 281.9 %collective-permute-start.1 = (bf16[1,7168,256]{2,1,0:T(8,128)(2,1)}, bf16[1,7168,256]{2,1,0:T(8,128)(2,1)}, u32[]{:S(2)}, u32[]{:S(2)}) collective-permute-start(bf16[1,7168,256]{2,1,0:T(8,128)(2,1)} %param.14), channel_id=1, source_target_pairs={{0,16},{1,17},{2,18},{3,19},{4,20},{5,21},{6,22},{7,23},{8,24},{9,... | collective-permute-start | bytes 11010056 | tf_op jit(solution)/shard_map/ppermute | solution.py:302
  138.0 283.6 %collective-permute-start = (bf16[1,7168,256]{2,1,0:T(8,128)(2,1)}, bf16[1,7168,256]{2,1,0:T(8,128)(2,1)}, u32[]{:S(2)}, u32[]{:S(2)}) collective-permute-start(bf16[1,7168,256]{2,1,0:T(8,128)(2,1)} %param.13), channel_id=1, source_target_pairs={{0,16},{1,17},{2,18},{3,19},{4,20},{5,21},{6,22},{7,23},{8,24},{9,... | collective-permute-start | bytes 11010056 | tf_op jit(solution)/shard_map/ppermute | solution.py:302
  414.9 4.5 %copy-start.1 = (bf16[1,7168,256]{2,1,0:T(8,128)(2,1)S(1)}, bf16[1,7168,256]{2,1,0:T(8,128)(2,1)}, u32[]{:S(2)}) copy-start(bf16[1,7168,256]{2,1,0:T(8,128)(2,1)} %param.14) | copy-start | bytes 11010052
  419.4 3.4 copy-start.2
Sparse Core Ops, SparseCore 0:
  136.1 67.9 all-gather.1

commit v2 on v1

v2 whole, which is shorter than its diff:
```python
import jax
import jax.numpy as jnp
from jax import lax
from jax.experimental import pallas as pl
from jax.experimental.pallas import tpu as pltpu
from jax.sharding import PartitionSpec as P

RING = 4


def wrap(value):
    return lax.rem(value + RING, RING)


def place():
    attn = lax.axis_index("attn")
    exp = lax.axis_index("exp")
    z_hi, core = attn // 2, lax.rem(attn, 2)
    z_lo, y, x = exp // 16, lax.rem(exp // 4, 4), lax.rem(exp, 4)
    return z_hi, core, z_lo, y, x


def device(z_hi, core, z_lo, y, x):
    return {"attn": z_hi * 2 + core, "exp": z_lo * 16 + y * 4 + x}


def neighbours(z_hi, core, z_lo, y, x):
    z = z_hi * 2 + z_lo
    right_z, left_z = wrap(z + 1), wrap(z - 1)
    along_z = [device(n // 2, core, lax.rem(n, 2), y, x) for n in (right_z, left_z)]
    along_x = [device(z_hi, core, z_lo, y, n) for n in (wrap(x + 1), wrap(x - 1))]
    along_y = [device(z_hi, core, z_lo, n, x) for n in (wrap(y + 1), wrap(y - 1))]
    return along_z, along_x, along_y, device(z_hi, 1 - core, z_lo, y, x)


def greet(devices):
    barrier = pltpu.get_barrier_semaphore()
    for other in devices:
        pl.semaphore_signal(barrier, inc=1, device_id=other, device_id_type=pl.DeviceIdType.MESH)
    pl.semaphore_wait(barrier, len(devices))


class Sends:
    def __init__(self, send_sem, recv_sem):
        self.send_sem, self.recv_sem, self.copies = send_sem, recv_sem, []

    def __call__(self, src, dst, to):
        k = len(self.copies)
        copy = pltpu.make_async_remote_copy(
            src_ref=src,
            dst_ref=dst,
            send_sem=self.send_sem.at[k],
            recv_sem=self.recv_sem.at[k],
            device_id=to,
            device_id_type=pl.DeviceIdType.MESH,
        )
        copy.start()
        self.copies.append(copy)
        return copy


STEPS = 2
PIECES = 16
EARLY, LATE = 20, 42
COPIES = 6 + 12 + 12 + 16 + 8 + 2 * (2 + 4 + 2 + 2) + 2
TILES = 8
EXTRA = 128


def layer_kernel(
    tok_ref, pick_ref, wg_ref, wu_ref, wd_ref,
    mixed_ref, og_ref, ou_ref, od_ref, all_ref,
    wg_v, wu_v, wd_v, tile_v, hall, relay, sel_v, wcol_v, c_v,
    hop0, got0, sum0, hop1, got1, sum1, last,
    local_sem, tile_sem, send_sem, recv_sem, swap_send, swap_recv,
):
    z_hi, core, z_lo, y, x = place()
    along_z, along_x, along_y, sibling = neighbours(z_hi, core, z_lo, y, x)
    partner = device(z_hi, core, 1 - z_lo, y, x)
    z = z_hi * 2 + z_lo
    attn = z_hi * 2 + core
    wide = tok_ref.shape[2]
    quarter = wide - EXTRA
    part = wg_ref.shape[1]
    send = Sends(send_sem, recv_sem)

    loads = [
        pltpu.make_async_copy(src, dst, local_sem.at[2 + k])
        for k, (src, dst) in enumerate(((wg_ref, wg_v), (wu_ref, wu_v), (wd_ref, wd_v)))
    ]
    for copy in loads:
        copy.start()
    greet(along_z + along_x + along_y + [sibling])

    swaps = []
    for src, dst in ((wg_ref, og_ref), (wu_ref, ou_ref), (wd_ref, od_ref)):
        size = src.shape[0] // PIECES
        for k in range(PIECES):
            n = len(swaps)
            swaps.append(
                pltpu.make_async_remote_copy(
                    src_ref=src.at[pl.ds(k * size, size)],
                    dst_ref=dst.at[pl.ds(k * size, size)],
                    send_sem=swap_send.at[n],
                    recv_sem=swap_recv.at[n],
                    device_id=partner,
                    device_id_type=pl.DeviceIdType.MESH,
                )
            )
    begun = [0]

    def swap_until(count):
        for copy in swaps[begun[0] : count]:
            copy.start()
        begun[0] = max(begun[0], count)

    def cols(high):
        return pl.ds(pl.multiple_of((high * 2 + core) * wide, 128), wide)

    def spot(step, at):
        return all_ref.at[step, lax.rem(at, 2), y, x, :, cols(at // 2)]

    own = [pltpu.make_async_copy(tok_ref.at[s], spot(s, z), local_sem.at[s]) for s in range(STEPS)]
    for copy in own:
        copy.start()
    first = {}
    for s in range(STEPS):
        for d in range(2):
            first[d, s] = send(tok_ref.at[s], spot(s, z), along_z[d])
    first[0, 0].wait_recv()
    forward0 = send(spot(0, wrap(z - 1)), spot(0, wrap(z - 1)), along_z[0])
    first[1, 1].wait_recv()
    forward1 = send(spot(1, wrap(z + 1)), spot(1, wrap(z + 1)), along_z[1])
    rest = {0: [first[1, 0], forward0], 1: [first[0, 1], forward1]}
    swap_until(EARLY)

    def line(step, axis, at, high):
        if axis == "x":
            return all_ref.at[step, :, y, at, :, cols(high)]
        return all_ref.at[step, :, at, x, :, cols(high)]

    def sheet(step, axis, at, high):
        if axis == "x":
            return all_ref.at[step, :, :, at, :, cols(high)]
        return all_ref.at[step, :, at, :, :, cols(high)]

    along = {"x": along_x, "y": along_y}
    spot_on = {"x": x, "y": y}
    order = (("x", "y"), ("y", "x"))

    def start_ring(unit, step, axis):
        at = spot_on[axis]
        return {
            (d, high): send(unit(step, axis, at, high), unit(step, axis, at, high), along[axis][d])
            for high in range(2)
            for d in range(2)
        }

    def forward_ring(copies, unit, step, axis):
        at = spot_on[axis]
        out = []
        for d in range(2):
            origin = wrap(at - 1) if d == 0 else wrap(at + 1)
            copies[d, d].wait_recv()
            out.append(send(unit(step, axis, origin, d), unit(step, axis, origin, d), along[axis][d]))
        return out

    lines, line_forwards = {}, {}
    for s in range(STEPS):
        for copy in rest[s]:
            copy.wait_recv()
        own[s].wait()
        lines[s] = start_ring(line, s, order[s][0])
    for s in range(STEPS):
        line_forwards[s] = forward_ring(lines[s], line, s, order[s][0])
    sheets, sheet_forwards, shared = {}, {}, []
    for s in range(STEPS):
        lines[s][0, 1].wait_recv()
        lines[s][1, 0].wait_recv()
        for copy in line_forwards[s]:
            copy.wait_recv()
        sheets[s] = start_ring(sheet, s, order[s][1])

    def share(step, offset, high):
        axis = order[step][1]
        unit = sheet(step, axis, wrap(spot_on[axis] + offset), high)
        shared.append(send(unit, unit, sibling))

    for s in range(STEPS):
        for high in range(2):
            share(s, 0, high)
    for s in range(STEPS):
        sheet_forwards[s] = forward_ring(sheets[s], sheet, s, order[s][1])
        share(s, -1, 0)
        share(s, 1, 1)
    for s in range(STEPS):
        sheets[s][0, 1].wait_recv()
        share(s, -1, 1)
        sheets[s][1, 0].wait_recv()
        share(s, 1, 0)
    for s in range(STEPS):
        for d in range(2):
            sheet_forwards[s][d].wait_recv()
            share(s, 2, d)
    for copy in shared:
        copy.wait_recv()
    for copy in loads:
        copy.wait()

    def tile_copy(t, slot):
        src = all_ref.at[t // 4, lax.rem(t // 2, 2), pl.ds(lax.rem(t, 2) * 2, 2)]
        return pltpu.make_async_copy(src, tile_v.at[slot], tile_sem.at[slot])

    span = tile_v.shape[1] * tile_v.shape[2] * tile_v.shape[3]
    slots = span // 2
    block = tile_v.shape[3]
    pick = pick_ref[...]

    tile_copy(0, 0).start()

    def gate_up(t, carry):
        slot = lax.rem(t, 2)
        tile_copy(t, slot).wait()

        @pl.when(t + 1 < TILES)
        def _():
            tile_copy(t + 1, 1 - slot).start()

        extra = tile_v[slot, :, :, :, quarter:wide].reshape(span, EXTRA)
        along_lanes = lax.dot_general(pick, extra, (((1,), (1,)), ((), ())), preferred_element_type=jnp.float32)
        mask = along_lanes > 0.0
        row_i = lax.broadcasted_iota(jnp.int32, (span, span), 0)
        col_i = lax.broadcasted_iota(jnp.int32, (span, span), 1)
        upto = jnp.where((row_i // block == col_i // block) & (row_i <= col_i), 1.0, 0.0).astype(jnp.bfloat16)
        count = jnp.dot(
            jnp.where(mask, 1.0, 0.0).astype(jnp.bfloat16), upto, preferred_element_type=jnp.float32
        )
        base = lax.broadcasted_iota(jnp.int32, count.shape, 1) // block * (block // 2) - 1
        where_to = jnp.where(mask, count + base.astype(jnp.float32), -1.0)[0:1, :]
        slot_i = lax.broadcasted_iota(jnp.int32, (slots, span), 0).astype(jnp.float32)
        sel = jnp.where(slot_i == where_to, 1.0, 0.0).astype(jnp.bfloat16)
        sel_v[t] = sel
        wcol = jnp.sum(extra.astype(jnp.float32) * pick[0:1].astype(jnp.float32), axis=1, keepdims=True)
        wcol_v[t] = jnp.broadcast_to(2.5 * wcol, (span, 128))
        gate = jnp.zeros((slots, part), jnp.float32)
        upper = jnp.zeros((slots, part), jnp.float32)
        for q in range(4):
            rows = tile_v[slot, :, :, :, q * wide : q * wide + quarter].reshape(span, quarter)
            served = jnp.dot(sel, rows, preferred_element_type=jnp.float32).astype(jnp.bfloat16)
            w = pl.ds(q * quarter, quarter)
            gate = gate + jnp.dot(served, wg_v[w, :], preferred_element_type=jnp.float32)
            upper = upper + jnp.dot(served, wu_v[w, :], preferred_element_type=jnp.float32)
        act = gate / (1.0 + jnp.exp(-gate)) * upper
        hall[attn, t] = act.astype(jnp.bfloat16)
        return carry

    lax.fori_loop(0, TILES, gate_up, 0)

    half = [pl.ds(0, TILES // 2), pl.ds(TILES // 2, TILES // 2)]
    hops = [send(hall.at[attn, half[d]], relay.at[d], along_z[d]) for d in range(2)]
    to_core = [send(hall.at[attn], hall.at[attn], sibling)]
    far = []
    for d in range(2):
        hops[d].wait_recv()
        origin = (wrap(z - 1) if d == 0 else wrap(z + 1)) // 2 * 2 + core
        far.append(send(relay.at[d], hall.at[origin, half[d]], along_z[d]))
    swap_until(LATE)
    opposite = (1 - z_hi) * 2 + core
    for d in range(2):
        far[d].wait_recv()
        to_core.append(send(hall.at[opposite, half[d]], hall.at[opposite, half[d]], sibling))
    for copy in to_core:
        copy.wait_recv()

    def down(t, carry):
        total = jnp.zeros((slots, quarter), jnp.float32)
        for a in range(4):
            total = total + jnp.dot(
                hall[a, t], wd_v[pl.ds(a * part, part), :], preferred_element_type=jnp.float32
            )
        produced = total.astype(jnp.bfloat16)
        spread = lax.dot_general(
            sel_v[t], produced, (((0,), (0,)), ((), ())), preferred_element_type=jnp.float32
        )
        scaled = (wcol_v[t][:, 0:1] * spread).astype(jnp.bfloat16)
        c_v[t // 4, lax.rem(t // 2, 2), pl.ds(lax.rem(t, 2) * 2, 2)] = scaled.reshape(c_v.shape[2] // 2, *c_v.shape[3:])
        return carry

    lax.fori_loop(0, TILES, down, 0)

    flow = (("y", "x"), ("x", "y"))

    def lane(step, at):
        if flow[step][0] == "y":
            return c_v.at[step, :, at]
        return c_v.at[step, :, :, at]

    hops, fulls = {}, {}
    for s in range(STEPS):
        axis = flow[s][0]
        at = spot_on[axis]
        hops[s] = [send(lane(s, wrap(at + 2)).at[d], hop0.at[s, d], along[axis][d]) for d in range(2)]
    for s in range(STEPS):
        axis = flow[s][0]
        at = spot_on[axis]
        for d in range(2):
            target = wrap(at + 1) if d == 0 else wrap(at - 1)
            fulls[s, d] = [send(lane(s, target).at[1 - d], got0.at[s, d, 1 - d], along[axis][d])]
    for s in range(STEPS):
        axis = flow[s][0]
        at = spot_on[axis]
        for d in range(2):
            target = wrap(at + 1) if d == 0 else wrap(at - 1)
            hops[s][d].wait_recv()
            mine = lane(s, target)

            @pl.loop(0, RING)
            def _(i, mine=mine, s=s, d=d):
                total = mine[d, i].astype(jnp.float32) + hop0[s, d, i].astype(jnp.float32)
                hop0[s, d, i] = total.astype(jnp.bfloat16)

            fulls[s, d].append(send(hop0.at[s, d], got0.at[s, d, d], along[axis][d]))
    hops1, fulls1 = {}, {}
    for s in range(STEPS):
        at = spot_on[flow[s][0]]
        mine = lane(s, at)
        for d in range(2):
            for copy in fulls[s, d]:
                copy.wait_recv()

        @pl.loop(0, RING)
        def _(i, mine=mine, s=s):
            for h in range(2):
                total = mine[h, i].astype(jnp.float32)
                total = total + got0[s, 0, h, i].astype(jnp.float32)
                total = total + got0[s, 1, h, i].astype(jnp.float32)
                sum0[s, h, i] = total

        axis = flow[s][1]
        at = spot_on[axis]
        hops1[s] = [send(sum0.at[s, d, wrap(at + 2)], hop1.at[s, d], along[axis][d]) for d in range(2)]
    for s in range(STEPS):
        axis = flow[s][1]
        at = spot_on[axis]
        for d in range(2):
            target = wrap(at + 1) if d == 0 else wrap(at - 1)
            hops1[s][d].wait_recv()
            sum0[s, d, target] = sum0[s, d, target] + hop1[s, d]
            fulls1[s, d] = send(sum0.at[s, :, target], got1.at[s, d], along[axis][d])
    finals = []
    for s in range(STEPS):
        at = spot_on[flow[s][1]]
        for d in range(2):
            fulls1[s, d].wait_recv()
        away = 1 - z_lo
        sum1[s] = (sum0[s, away, at] + got1[s, 0, away] + got1[s, 1, away]).astype(jnp.bfloat16)
        finals.append(send(sum1.at[s], last.at[s], partner))
    swap_until(3 * PIECES)
    for s in range(STEPS):
        at = spot_on[flow[s][1]]
        finals[s].wait_recv()
        total = sum0[s, z_lo, at] + got1[s, 0, z_lo] + got1[s, 1, z_lo] + last[s].astype(jnp.float32)
        mixed_ref[s] = total.astype(jnp.bfloat16)
    for copy in send.copies:
        copy.wait_send()
    for copy in swaps:
        copy.wait()


def layer(tokens, pick, w_gate, w_up, w_down):
    steps, rows, wide = tokens.shape
    quarter = wide - EXTRA
    dt = tokens.dtype
    part = w_gate.shape[1]
    plane = (2, RING, RING, rows)
    hbm = pl.BlockSpec(memory_space=pl.ANY)
    vmem = pl.BlockSpec(memory_space=pltpu.VMEM)
    like = lambda a: jax.ShapeDtypeStruct(a.shape, a.dtype)
    return pl.pallas_call(
        layer_kernel,
        out_shape=(
            jax.ShapeDtypeStruct((steps, rows, quarter), dt),
            like(w_gate),
            like(w_up),
            like(w_down),
            jax.ShapeDtypeStruct((steps, *plane, 4 * wide), dt),
        ),
        in_specs=[hbm, vmem, hbm, hbm, hbm],
        out_specs=(vmem, hbm, hbm, hbm, hbm),
        scratch_shapes=[
            pltpu.VMEM(w_gate.shape, dt),
            pltpu.VMEM(w_up.shape, dt),
            pltpu.VMEM(w_down.shape, dt),
            pltpu.VMEM((2, 2, RING, rows, 4 * wide), dt),
            pltpu.VMEM((4, TILES, 4 * rows, part), dt),
            pltpu.VMEM((2, TILES // 2, 4 * rows, part), dt),
            pltpu.VMEM((TILES, 4 * rows, 8 * rows), dt),
            pltpu.VMEM((TILES, 8 * rows, 128), jnp.float32),
            pltpu.VMEM((steps, *plane, quarter), dt),
            pltpu.VMEM((steps, 2, RING, rows, quarter), dt),
            pltpu.VMEM((steps, 2, 2, RING, rows, quarter), dt),
            pltpu.VMEM((steps, 2, RING, rows, quarter), jnp.float32),
            pltpu.VMEM((steps, 2, rows, quarter), jnp.float32),
            pltpu.VMEM((steps, 2, 2, rows, quarter), jnp.float32),
            pltpu.VMEM((steps, rows, quarter), dt),
            pltpu.VMEM((steps, rows, quarter), dt),
            pltpu.SemaphoreType.DMA((5,)),
            pltpu.SemaphoreType.DMA((2,)),
            pltpu.SemaphoreType.DMA((COPIES,)),
            pltpu.SemaphoreType.DMA((COPIES,)),
            pltpu.SemaphoreType.DMA((3 * PIECES,)),
            pltpu.SemaphoreType.DMA((3 * PIECES,)),
        ],
        compiler_params=pltpu.CompilerParams(
            collective_id=0, has_side_effects=True, vmem_limit_bytes=58 * 1024 * 1024
        ),
        name="layer",
    )(tokens, pick, w_gate, w_up, w_down)[:4]


def three_parts(value):
    parts = []
    for _ in range(3):
        part = lax.reduce_precision(value, exponent_bits=8, mantissa_bits=7)
        parts.append(part.astype(jnp.bfloat16))
        value = value - part
    return parts


def per_device(tokens, logits, routes, held, swapped, w_gate, w_up, w_down):
    exp_count = lax.axis_size("exp")
    own_index = lax.axis_index("exp")
    own_flag = swapped[own_index % (exp_count // 2)]

    score = jax.nn.sigmoid(logits)
    weight = score / jnp.sum(score, axis=-1, keepdims=True)
    expert_ids = jnp.arange(exp_count, dtype=jnp.int32)
    named = routes[:, :, :, None] == expert_ids
    table = jnp.sum(jnp.where(named, weight[:, :, :, None], 0.0), axis=2)
    parts = three_parts(table)
    beside = jnp.concatenate([tokens, *parts, jnp.zeros_like(parts[0])], axis=2)
    lanes = jnp.arange(EXTRA, dtype=jnp.int32)
    own_expert = held[own_index]
    picked = (lanes % exp_count == own_expert) & (lanes < 3 * exp_count)
    pick = jnp.broadcast_to(picked.astype(jnp.bfloat16)[None, :], (16, EXTRA))

    mixed, *others = layer(beside, pick, w_gate[0], w_up[0], w_down[0])
    afters = [
        jnp.where(own_flag == 1, other[None], w) for other, w in zip(others, (w_gate, w_up, w_down))
    ]
    return (mixed, *afters)


def solution(mesh):
    in_specs = (
        P(None, "exp", "attn"),
        P(None, "exp", None),
        P(None, "exp", None),
        P(),
        P(),
        P("exp", None, "attn"),
        P("exp", None, "attn"),
        P("exp", None, "attn"),
    )
    out_specs = (
        P(None, "exp", "attn"),
        P("exp", None, "attn"),
        P("exp", None, "attn"),
        P("exp", None, "attn"),
    )
    return jax.shard_map(
        per_device, mesh=mesh, in_specs=in_specs, out_specs=out_specs, check_vma=False
    )
```

time: 433 us -> 307 us (0.71)
  blocking collectives: 85.7 us -> 0 us
  matrix products: 40 us -> 0 us
  between operations: 14.9 us -> 1.36 us
  other arithmetic: 10.1 us -> 16.3 us
    all_gather x1 -> x0, blocking collectives: 85.7 us -> none  [per_device(): everyone = lax.all_gather(table, 'exp', axis=1, tiled=True)]
    dot_general x3 -> x0, matrix products: 40 us -> none  [the longest x1 14.9 us: per_device(): upper = jnp.dot(rows, up_tile, preferred_element_type=jnp.float32)]
    select_n x3 -> x2, other arithmetic: 8.9 us -> 14 us  [per_device(): jnp.where(own_flag == 1, other[None], w)]
    pallas_call x2 -> x1, Pallas kernels: 275 us -> 279 us  [layer(): pl.pallas_call(layer_kernel, out_shape=(jax.ShapeDtypeStruct((steps, rows...]
  transfers between devices with their start and end apart: 4 -> 0, of which waited for: 0 -> 0; matrix products, arithmetic and copies ran while one was open for 5% -> 0% of each run, Pallas kernels for 41% -> 0%
where the time goes in v2:
time: 307 us; the launch traced here: 303 us
  Pallas kernels  279 us (91%)
  other arithmetic  16.3 us (5%)
  local copies, waits for them, and re-layouts  6.38 us (2%)
    pallas_call x1, Pallas kernels, layer(): pl.pallas_call(layer_kernel, out_shape=(jax.ShapeDtypeStruct((steps, rows...  279 us
    select_n x2, other arithmetic, per_device(): jnp.where(own_flag == 1, other[None], w)  14 us

profile of v2, /device:TPU:0, one launch (start us, length us, event | category | flops | bytes accessed | tf_op | source)
XLA Modules:
  0.0 303.0 jit_solution(17972566452268675032)
XLA Ops:
  0.6 1.2 dynamic_slice.7
  2.5 1.2 dynamic_slice.6
  3.8 0.6 and_convert_fusion
  4.4 0.7 divide_reduce_fusion
  5.2 0.6 broadcast_in_dim.37.pick_ref
  5.8 0.7 multiply_divide_fusion
  6.5 0.1 copy.15
  6.5 0.8 copy.14
  7.3 0.2 select_reduce_fusion
  7.6 1.7 concatenate.3.tok_ref
  9.3 279.0 %layer.1 = (bf16[2,32,1792]{2,1,0:T(8,128)(2,1)}, bf16[7168,256]{1,0:T(8,128)(2,1)}, bf16[7168,256]{1,0:T(8,128)(2,1)}, bf16[1024,1792]{1,0:T(8,128)(2,1)}, bf16[2,2,4,4,32,7680]{5,4,3,2,1,0:T(8,128)(2,1)}) custom-call(bf16[2,32,1920]{2,1,0:T(8,128)(2,1)} %concatenate.3.tok_ref, bf16[16,128]{1,0:T(8,128)(2,1)} %broadcast_in_dim.37.pick_ref, ...), custom_call_target="tpu_custom_call" | custom-call | tf_op jit(solution)/shard_map/layer/pallas_call | solution.py:379
  288.3 0.0 copy-start
  288.4 5.5 %bitcast_select_fusion = bf16[1,1024,1792]{2,1,0:T(8,128)(2,1)} fusion(bf16[1,1024,1792]{2,1,0:T(8,128)(2,1)} %param.15, bf16[1024,1792]{1,0:T(8,128)(2,1)} %get-tuple-element.11, pred[]{:T(512)} %bitcast.4), kind=kLoop, calls=%fused_computation | loop fusion | flops 1835008 | bytes 11010049 | tf_op jit(solution)/shard_map/jit(_where)/select_n | solution.py:449
  293.9 0.0 copy-done
  293.9 0.0 copy-start.1
  293.9 8.5 %bitcast_select_fusion.1 = (bf16[1,7168,256]{2,1,0:T(8,128)(2,1)}, bf16[1,7168,256]{2,1,0:T(8,128)(2,1)}) fusion(bf16[1,7168,256]{2,1,0:T(8,128)(2,1)} %param.14, bf16[7168,256]{1,0:T(8,128)(2,1)} %get-tuple-element.10, pred[]{:T(512)} %bitcast.4, bf16[1,7168,256]{2,1,0:T(8,128)(2,1)S(1)} %copy-done, bf16[7168,256]{1,0:T(8,128)(2,1)} %get-tuple-element.9), kind=kLoop, calls=%fused_computation.1 | loop fusion | flops 3670016 | bytes 22020096 | tf_op jit(solution)/shard_map/jit(_where)/select_n | solution.py:449
  302.3 0.0 copy-done.1
  302.3 0.7 copy.17
  (2 shorter events, 0.0 us)
Async XLA Ops:
  288.3 5.5 %copy-start = (bf16[1,7168,256]{2,1,0:T(8,128)(2,1)S(1)}, bf16[1,7168,256]{2,1,0:T(8,128)(2,1)}, u32[]{:S(2)}) copy-start(bf16[1,7168,256]{2,1,0:T(8,128)(2,1)} %param.13) | copy-start | bytes 11010052
  293.9 8.5 %copy-start.1 = (bf16[2,32,1792]{2,1,0:T(8,128)(2,1)S(1)}, bf16[2,32,1792]{2,1,0:T(8,128)(2,1)}, u32[]{:S(2)}) copy-start(bf16[2,32,1792]{2,1,0:T(8,128)(2,1)} %get-tuple-element.21) | copy-start | bytes 688132

commit v3 on v2

--- a/solution.py
+++ b/solution.py
@@ -1,3 +1,5 @@
+import functools
+
 import jax
 import jax.numpy as jnp
 from jax import lax
@@ -61,16 +63,17 @@
 
 STEPS = 2
 PIECES = 16
-EARLY, LATE = 20, 42
+SLAB = 64
+EARLY, LATE = 26, 41
 COPIES = 6 + 12 + 12 + 16 + 8 + 2 * (2 + 4 + 2 + 2) + 2
 TILES = 8
 EXTRA = 128
 
 
 def layer_kernel(
-    tok_ref, pick_ref, wg_ref, wu_ref, wd_ref,
+    held_ref, swapped_ref, tokens_ref, logits_ref, routes_ref, wg_ref, wu_ref, wd_ref,
     mixed_ref, og_ref, ou_ref, od_ref, all_ref,
-    wg_v, wu_v, wd_v, tile_v, hall, relay, sel_v, wcol_v, c_v,
+    wg_v, wu_v, wd_v, tok_ref, tile_v, hall, relay, sel_v, wcol_v,
     hop0, got0, sum0, hop1, got1, sum1, last,
     local_sem, tile_sem, send_sem, recv_sem, swap_send, swap_recv,
 ):
@@ -88,7 +91,8 @@
         pltpu.make_async_copy(src, dst, local_sem.at[2 + k])
         for k, (src, dst) in enumerate(((wg_ref, wg_v), (wu_ref, wu_v), (wd_ref, wd_v)))
     ]
-    for copy in loads:
+    tok_load = pltpu.make_async_copy(tokens_ref, tok_ref.at[:, :, pl.ds(0, quarter)], local_sem.at[5])
+    for copy in [tok_load, *loads]:
         copy.start()
     greet(along_z + along_x + along_y + [sibling])
 
@@ -120,19 +124,36 @@
     def spot(step, at):
         return all_ref.at[step, lax.rem(at, 2), y, x, :, cols(at // 2)]
 
+    exp_count = held_ref.shape[0]
+    lane_i = lax.broadcasted_iota(jnp.int32, (logits_ref.shape[1], EXTRA), 1)
+    expert_i = lax.rem(lane_i, exp_count)
+    for s in range(STEPS):
+        score = 1.0 / (1.0 + jnp.exp(-logits_ref[s]))
+        weight = score / jnp.sum(score, axis=1, keepdims=True)
+        names = routes_ref[s]
+        table = jnp.zeros(lane_i.shape, jnp.float32)
+        for k in range(names.shape[1]):
+            table = table + jnp.where(names[:, k : k + 1] == expert_i, weight[:, k : k + 1], 0.0)
+        high = table.astype(jnp.bfloat16).astype(jnp.float32)
+        middle = (table - high).astype(jnp.bfloat16).astype(jnp.float32)
+        low = table - high - middle
+        parts = jnp.where(lane_i < exp_count, high, jnp.where(lane_i < 2 * exp_count, middle, low))
+        parts = jnp.where(lane_i < 3 * exp_count, parts, 0.0)
+        tok_ref[s, :, quarter:wide] = parts.astype(jnp.bfloat16)
+    tok_load.wait()
+
     own = [pltpu.make_async_copy(tok_ref.at[s], spot(s, z), local_sem.at[s]) for s in range(STEPS)]
     for copy in own:
         copy.start()
-    first = {}
-    for s in range(STEPS):
-        for d in range(2):
-            first[d, s] = send(tok_ref.at[s], spot(s, z), along_z[d])
-    first[0, 0].wait_recv()
-    forward0 = send(spot(0, wrap(z - 1)), spot(0, wrap(z - 1)), along_z[0])
-    first[1, 1].wait_recv()
-    forward1 = send(spot(1, wrap(z + 1)), spot(1, wrap(z + 1)), along_z[1])
-    rest = {0: [first[1, 0], forward0], 1: [first[0, 1], forward1]}
+    beyond = wrap(z + 2 * z_lo - 1)
+    beyond_device = device(beyond // 2, core, lax.rem(beyond, 2), y, x)
+    near = [send(tok_ref.at[s], spot(s, z), partner) for s in range(STEPS)]
     swap_until(EARLY)
+    rest = {s: [send(tok_ref.at[s], spot(s, z), beyond_device)] for s in range(STEPS)}
+    pair = z + 1 - 2 * z_lo
+    for s in range(STEPS):
+        near[s].wait_recv()
+        rest[s].append(send(spot(s, pair), spot(s, pair), beyond_device))
 
     def line(step, axis, at, high):
         if axis == "x":
@@ -214,7 +235,11 @@
     span = tile_v.shape[1] * tile_v.shape[2] * tile_v.shape[3]
     slots = span // 2
     block = tile_v.shape[3]
-    pick = pick_ref[...]
+    own_expert = held_ref[lax.axis_index("exp")]
+    pick_i = lax.broadcasted_iota(jnp.int32, (16, EXTRA), 1)
+    pick = jnp.where(
+        (lax.rem(pick_i, exp_count) == own_expert) & (pick_i < 3 * exp_count), 1.0, 0.0
+    ).astype(jnp.bfloat16)
 
     tile_copy(0, 0).start()
 
@@ -272,7 +297,7 @@
     for copy in to_core:
         copy.wait_recv()
 
-    def down(t, carry):
+    def down(step, t, carry):
         total = jnp.zeros((slots, quarter), jnp.float32)
         for a in range(4):
             total = total + jnp.dot(
@@ -283,17 +308,24 @@
             sel_v[t], produced, (((0,), (0,)), ((), ())), preferred_element_type=jnp.float32
         )
         scaled = (wcol_v[t][:, 0:1] * spread).astype(jnp.bfloat16)
-        c_v[t // 4, lax.rem(t // 2, 2), pl.ds(lax.rem(t, 2) * 2, 2)] = scaled.reshape(c_v.shape[2] // 2, *c_v.shape[3:])
+        scaled = scaled.reshape(2, RING, block, quarter)
+        low = lax.rem(t // 2, 2)
+        for k in range(2):
+            row = lax.rem(t, 2) * 2 + k
+            if step == 0:
+                tile_v[0, low, :, :, pl.ds(pl.multiple_of(row * quarter, 128), quarter)] = scaled[k]
+            else:
+                for i in range(RING):
+                    tile_v[1, low, row, :, i * quarter : (i + 1) * quarter] = scaled[k, i]
         return carry
 
-    lax.fori_loop(0, TILES, down, 0)
+    for step in range(STEPS):
+        lax.fori_loop(step * TILES // 2, (step + 1) * TILES // 2, functools.partial(down, step), 0)
 
     flow = (("y", "x"), ("x", "y"))
 
     def lane(step, at):
-        if flow[step][0] == "y":
-            return c_v.at[step, :, at]
-        return c_v.at[step, :, :, at]
+        return tile_v.at[step, :, :, :, pl.ds(pl.multiple_of(at * quarter, 128), quarter)]
 
     hops, fulls = {}, {}
     for s in range(STEPS):
@@ -361,20 +393,33 @@
         finals[s].wait_recv()
         total = sum0[s, z_lo, at] + got1[s, 0, z_lo] + got1[s, 1, z_lo] + last[s].astype(jnp.float32)
         mixed_ref[s] = total.astype(jnp.bfloat16)
-    for copy in send.copies:
+    flag = swapped_ref[lax.rem(lax.axis_index("exp"), swapped_ref.shape[0])]
+    n = 0
+    for dst, src in ((og_ref, wg_v), (ou_ref, wu_v), (od_ref, wd_v)):
+        size = src.shape[0] // PIECES
+        for k in range(PIECES):
+            swaps[n].wait_recv()
+
+            @pl.loop(0, size // SLAB)
+            def _(i, dst=dst, src=src, k=k, size=size):
+                at = pl.ds(pl.multiple_of(k * size + i * SLAB, SLAB), SLAB)
+                trade = jnp.full((SLAB, src.shape[1]), flag, jnp.int32) == 1
+                dst[at, :] = jnp.where(trade, dst[at, :], src[at, :])
+
+            n += 1
+    for copy in send.copies + swaps:
         copy.wait_send()
-    for copy in swaps:
-        copy.wait()
-
-
-def layer(tokens, pick, w_gate, w_up, w_down):
-    steps, rows, wide = tokens.shape
-    quarter = wide - EXTRA
+
+
+def layer(held, swapped, tokens, logits, routes, w_gate, w_up, w_down):
+    steps, rows, quarter = tokens.shape
+    wide = quarter + EXTRA
     dt = tokens.dtype
     part = w_gate.shape[1]
     plane = (2, RING, RING, rows)
     hbm = pl.BlockSpec(memory_space=pl.ANY)
     vmem = pl.BlockSpec(memory_space=pltpu.VMEM)
+    smem = pl.BlockSpec(memory_space=pltpu.SMEM)
     like = lambda a: jax.ShapeDtypeStruct(a.shape, a.dtype)
     return pl.pallas_call(
         layer_kernel,
@@ -385,18 +430,18 @@
             like(w_down),
             jax.ShapeDtypeStruct((steps, *plane, 4 * wide), dt),
         ),
-        in_specs=[hbm, vmem, hbm, hbm, hbm],
-        out_specs=(vmem, hbm, hbm, hbm, hbm),
+        in_specs=[smem, smem, hbm, vmem, vmem, hbm, hbm, hbm],
+        out_specs=(vmem, vmem, vmem, vmem, hbm),
         scratch_shapes=[
             pltpu.VMEM(w_gate.shape, dt),
             pltpu.VMEM(w_up.shape, dt),
             pltpu.VMEM(w_down.shape, dt),
+            pltpu.VMEM((steps, rows, wide), dt),
             pltpu.VMEM((2, 2, RING, rows, 4 * wide), dt),
             pltpu.VMEM((4, TILES, 4 * rows, part), dt),
             pltpu.VMEM((2, TILES // 2, 4 * rows, part), dt),
             pltpu.VMEM((TILES, 4 * rows, 8 * rows), dt),
             pltpu.VMEM((TILES, 8 * rows, 128), jnp.float32),
-            pltpu.VMEM((steps, *plane, quarter), dt),
             pltpu.VMEM((steps, 2, RING, rows, quarter), dt),
             pltpu.VMEM((steps, 2, 2, RING, rows, quarter), dt),
             pltpu.VMEM((steps, 2, RING, rows, quarter), jnp.float32),
@@ -404,7 +449,7 @@
             pltpu.VMEM((steps, 2, 2, rows, quarter), jnp.float32),
             pltpu.VMEM((steps, rows, quarter), dt),
             pltpu.VMEM((steps, rows, quarter), dt),
-            pltpu.SemaphoreType.DMA((5,)),
+            pltpu.SemaphoreType.DMA((6,)),
             pltpu.SemaphoreType.DMA((2,)),
             pltpu.SemaphoreType.DMA((COPIES,)),
             pltpu.SemaphoreType.DMA((COPIES,)),
@@ -412,43 +457,15 @@
             pltpu.SemaphoreType.DMA((3 * PIECES,)),
         ],
         compiler_params=pltpu.CompilerParams(
-            collective_id=0, has_side_effects=True, vmem_limit_bytes=58 * 1024 * 1024
+            collective_id=0, has_side_effects=True, vmem_limit_bytes=42 * 1024 * 1024
         ),
         name="layer",
-    )(tokens, pick, w_gate, w_up, w_down)[:4]
-
-
-def three_parts(value):
-    parts = []
-    for _ in range(3):
-        part = lax.reduce_precision(value, exponent_bits=8, mantissa_bits=7)
-        parts.append(part.astype(jnp.bfloat16))
-        value = value - part
-    return parts
+    )(held, swapped, tokens, logits, routes, w_gate, w_up, w_down)[:4]
 
 
 def per_device(tokens, logits, routes, held, swapped, w_gate, w_up, w_down):
-    exp_count = lax.axis_size("exp")
-    own_index = lax.axis_index("exp")
-    own_flag = swapped[own_index % (exp_count // 2)]
-
-    score = jax.nn.sigmoid(logits)
-    weight = score / jnp.sum(score, axis=-1, keepdims=True)
-    expert_ids = jnp.arange(exp_count, dtype=jnp.int32)
-    named = routes[:, :, :, None] == expert_ids
-    table = jnp.sum(jnp.where(named, weight[:, :, :, None], 0.0), axis=2)
-    parts = three_parts(table)
-    beside = jnp.concatenate([tokens, *parts, jnp.zeros_like(parts[0])], axis=2)
-    lanes = jnp.arange(EXTRA, dtype=jnp.int32)
-    own_expert = held[own_index]
-    picked = (lanes % exp_count == own_expert) & (lanes < 3 * exp_count)
-    pick = jnp.broadcast_to(picked.astype(jnp.bfloat16)[None, :], (16, EXTRA))
-
-    mixed, *others = layer(beside, pick, w_gate[0], w_up[0], w_down[0])
-    afters = [
-        jnp.where(own_flag == 1, other[None], w) for other, w in zip(others, (w_gate, w_up, w_down))
-    ]
-    return (mixed, *afters)
+    mixed, *tiles = layer(held, swapped, tokens, logits, routes, w_gate[0], w_up[0], w_down[0])
+    return (mixed, *(tile[None] for tile in tiles))
 
 
 def solution(mesh):

time: 307 us -> 278 us (0.906); the launches traced: 303 us -> 278 us
  other arithmetic: 16.3 us -> 0 us
  Pallas kernels: 279 us -> 267 us
  local copies, waits for them, and re-layouts: 6.38 us -> 10 us
    select_n x2 -> x0, other arithmetic: 14 us -> none  [per_device(): jnp.where(own_flag == 1, other[None], w)]
    pallas_call x1, Pallas kernels: 279 us -> 267 us  [layer(): pl.pallas_call(layer_kernel, out_shape=(jax.ShapeDtypeStruct((steps, rows...]
    unnamed x6 -> x12, local copies, waits for them, and re-layouts: 1.49 us -> 10 us
where the time goes in v3:
time: 278 us
  Pallas kernels  267 us (96%)
  local copies, waits for them, and re-layouts  10 us (4%)
    pallas_call x1, Pallas kernels, layer(): pl.pallas_call(layer_kernel, out_shape=(jax.ShapeDtypeStruct((steps, rows...  267 us
    unnamed x12, local copies, waits for them, and re-layouts  10 us

profile of v3, /device:TPU:0, one launch (start us, length us, event | category | flops | bytes accessed | tf_op | source)
XLA Modules:
  0.0 277.9 jit_solution(16892556154590032564)
XLA Ops:
  0.6 0.8 copy.12.logits_ref
  1.4 0.8 copy.13.routes_ref
  2.2 0.0 copy-start
  2.2 0.9 copy-done
  3.1 0.0 copy-start.1
  3.1 0.7 copy-done.1
  3.8 0.0 copy-start.2
  3.8 0.7 copy-done.2
  4.4 267.2 %layer.1 = (bf16[2,32,1792]{2,1,0:T(8,128)(2,1)S(1)}, bf16[7168,256]{1,0:T(8,128)(2,1)S(1)}, bf16[7168,256]{1,0:T(8,128)(2,1)S(1)}, bf16[1024,1792]{1,0:T(8,128)(2,1)S(1)}, bf16[2,2,4,4,32,7680]{5,4,3,2,1,0:T(8,128)(2,1)}) custom-call(s32[32]{0:T(128)S(1)} %copy-done.1, s32[16]{0:T(128)S(1)} %copy-done.2, bf16[2,32,1792]{2,1,0:T(8,128)(2,1)S(1)} %copy-done, ...), custom_call_target="tpu_custom_call" | custom-call | tf_op jit(solution)/shard_map/layer/pallas_call | solution.py:424
  271.7 0.7 copy.18
  272.4 1.8 copy.19
  274.2 1.8 copy.20
  276.0 1.8 copy.21
Async XLA Ops:
  2.2 0.9 copy-start
  3.1 0.7 copy-start.1
  3.8 0.7 copy-start.2

commit v4 on v3

--- a/solution.py
+++ b/solution.py
@@ -64,7 +64,7 @@
 STEPS = 2
 PIECES = 16
 SLAB = 64
-EARLY, LATE = 26, 41
+FIRST, EARLY, BETWEEN, LATE = 0, 30, 31, 46
 COPIES = 6 + 12 + 12 + 16 + 8 + 2 * (2 + 4 + 2 + 2) + 2
 TILES = 8
 EXTRA = 128
@@ -124,22 +124,28 @@
     def spot(step, at):
         return all_ref.at[step, lax.rem(at, 2), y, x, :, cols(at // 2)]
 
+    swap_until(FIRST)
+
     exp_count = held_ref.shape[0]
-    lane_i = lax.broadcasted_iota(jnp.int32, (logits_ref.shape[1], EXTRA), 1)
+    top, here = logits_ref.shape[1:]
+    lane_i = lax.broadcasted_iota(jnp.int32, (EXTRA, here), 0)
     expert_i = lax.rem(lane_i, exp_count)
+    unit = lax.broadcasted_iota(jnp.int32, (here, here), 0) == lax.broadcasted_iota(jnp.int32, (here, here), 1)
+    unit = jnp.where(unit, 1.0, 0.0).astype(jnp.bfloat16)
     for s in range(STEPS):
         score = 1.0 / (1.0 + jnp.exp(-logits_ref[s]))
-        weight = score / jnp.sum(score, axis=1, keepdims=True)
+        weight = score / jnp.sum(score, axis=0, keepdims=True)
         names = routes_ref[s]
         table = jnp.zeros(lane_i.shape, jnp.float32)
-        for k in range(names.shape[1]):
-            table = table + jnp.where(names[:, k : k + 1] == expert_i, weight[:, k : k + 1], 0.0)
+        for k in range(top):
+            table = table + jnp.where(names[k : k + 1, :] == expert_i, weight[k : k + 1, :], 0.0)
         high = table.astype(jnp.bfloat16).astype(jnp.float32)
         middle = (table - high).astype(jnp.bfloat16).astype(jnp.float32)
         low = table - high - middle
         parts = jnp.where(lane_i < exp_count, high, jnp.where(lane_i < 2 * exp_count, middle, low))
-        parts = jnp.where(lane_i < 3 * exp_count, parts, 0.0)
-        tok_ref[s, :, quarter:wide] = parts.astype(jnp.bfloat16)
+        parts = jnp.where(lane_i < 3 * exp_count, parts, 0.0).astype(jnp.bfloat16)
+        turned = lax.dot_general(unit, parts, (((1,), (1,)), ((), ())), preferred_element_type=jnp.float32)
+        tok_ref[s, :, quarter:wide] = turned.astype(jnp.bfloat16)
     tok_load.wait()
 
     own = [pltpu.make_async_copy(tok_ref.at[s], spot(s, z), local_sem.at[s]) for s in range(STEPS)]
@@ -284,6 +290,7 @@
     half = [pl.ds(0, TILES // 2), pl.ds(TILES // 2, TILES // 2)]
     hops = [send(hall.at[attn, half[d]], relay.at[d], along_z[d]) for d in range(2)]
     to_core = [send(hall.at[attn], hall.at[attn], sibling)]
+    swap_until(BETWEEN)
     far = []
     for d in range(2):
         hops[d].wait_recv()
@@ -430,7 +437,7 @@
             like(w_down),
             jax.ShapeDtypeStruct((steps, *plane, 4 * wide), dt),
         ),
-        in_specs=[smem, smem, hbm, vmem, vmem, hbm, hbm, hbm],
+        in_specs=[smem, smem, pl.BlockSpec(memory_space=pltpu.HBM), vmem, vmem, hbm, hbm, hbm],
         out_specs=(vmem, vmem, vmem, vmem, hbm),
         scratch_shapes=[
             pltpu.VMEM(w_gate.shape, dt),
@@ -463,8 +470,41 @@
     )(held, swapped, tokens, logits, routes, w_gate, w_up, w_down)[:4]
 
 
+STORES = 2
+
+
+def store_kernel(*refs):
+    count = (len(refs) - 1) // 2
+    sems = refs[-1]
+    copies = []
+    for k in range(count):
+        src, dst = refs[k], refs[count + k]
+        size = src.shape[0] // STORES
+        for i in range(STORES):
+            rows = pl.ds(i * size, size)
+            copies.append(pltpu.make_async_copy(src.at[rows], dst.at[rows], sems.at[len(copies)]))
+    for copy in copies:
+        copy.start()
+    for copy in copies:
+        copy.wait()
+
+
+def store(*arrays):
+    return pl.pallas_call(
+        store_kernel,
+        out_shape=tuple(jax.ShapeDtypeStruct(a.shape, a.dtype) for a in arrays),
+        in_specs=[pl.BlockSpec(memory_space=pltpu.VMEM)] * len(arrays),
+        out_specs=(pl.BlockSpec(memory_space=pl.ANY),) * len(arrays),
+        scratch_shapes=[pltpu.SemaphoreType.DMA((STORES * len(arrays),))],
+        compiler_params=pltpu.CompilerParams(vmem_limit_bytes=16 * 1024 * 1024),
+        name="store",
+    )(*arrays)
+
+
 def per_device(tokens, logits, routes, held, swapped, w_gate, w_up, w_down):
-    mixed, *tiles = layer(held, swapped, tokens, logits, routes, w_gate[0], w_up[0], w_down[0])
+    by_choice = (jnp.swapaxes(logits, 1, 2), jnp.swapaxes(routes, 1, 2))
+    mixed, *tiles = layer(held, swapped, tokens, *by_choice, w_gate[0], w_up[0], w_down[0])
+    mixed, *tiles = store(mixed, *tiles)
     return (mixed, *(tile[None] for tile in tiles))
 
 

time: 278 us -> 275 us (0.989)
  local copies, waits for them, and re-layouts: 10 us -> 3.63 us
  Pallas kernels: 267 us -> 271 us
    unnamed x12 -> x10, local copies, waits for them, and re-layouts: 10 us -> 3.63 us
    pallas_call x0 -> x1, Pallas kernels: none -> 4.29 us  [store(): pl.pallas_call(store_kernel, out_shape=tuple((jax.ShapeDtypeStruct(a.shap...]
where the time goes in v4:
time: 275 us
  Pallas kernels  271 us (99%)
  local copies, waits for them, and re-layouts  3.63 us (1%)
    pallas_call x1, Pallas kernels, layer(): pl.pallas_call(layer_kernel, out_shape=(jax.ShapeDtypeStruct((steps, rows...  266 us

profile of v4, /device:TPU:0, one launch (start us, length us, event | category | flops | bytes accessed | tf_op | source)
XLA Modules:
  0.0 274.8 jit_solution(4193920116029442907)
XLA Ops:
  0.6 0.0 copy-start
  0.6 0.9 copy-done
  1.6 0.0 copy-start.1
  1.6 0.7 copy-done.1
  2.3 0.0 copy-start.2
  2.3 0.7 copy-done.2
  3.0 0.0 copy-start.3
  3.0 0.7 copy-done.3
  3.6 0.0 copy-start.4
  3.6 0.7 copy-done.4
  4.3 266.2 %layer.1 = (bf16[2,32,1792]{2,1,0:T(8,128)(2,1)S(1)}, bf16[7168,256]{1,0:T(8,128)(2,1)S(1)}, bf16[7168,256]{1,0:T(8,128)(2,1)S(1)}, bf16[1024,1792]{1,0:T(8,128)(2,1)S(1)}, bf16[2,2,4,4,32,7680]{5,4,3,2,1,0:T(8,128)(2,1)}) custom-call(s32[32]{0:T(128)S(1)} %copy-done.3, s32[16]{0:T(128)S(1)} %copy-done.4, bf16[2,32,1792]{2,1,0:T(8,128)(2,1)S(1)} %copy-done, ...), custom_call_target="tpu_custom_call" | custom-call | tf_op jit(solution)/shard_map/layer/pallas_call | solution.py:431
  270.5 4.3 %store.1 = (bf16[2,32,1792]{2,1,0:T(8,128)(2,1)}, bf16[7168,256]{1,0:T(8,128)(2,1)}, bf16[7168,256]{1,0:T(8,128)(2,1)}, bf16[1024,1792]{1,0:T(8,128)(2,1)}) custom-call(bf16[2,32,1792]{2,1,0:T(8,128)(2,1)S(1)} %get-tuple-element.12.refs_0_, bf16[7168,256]{1,0:T(8,128)(2,1)S(1)} %get-tuple-element.13.refs_1_, ...), custom_call_target="tpu_custom_call" | custom-call | tf_op jit(solution)/shard_map/store/pallas_call | solution.py:493
Async XLA Ops:
  0.6 0.9 copy-start
  1.6 0.7 copy-start.1
  2.3 0.7 copy-start.2
  3.0 0.7 copy-start.3
  3.6 0.7 copy-start.4

commit v5 on v4

--- a/solution.py
+++ b/solution.py
@@ -64,16 +64,16 @@
 STEPS = 2
 PIECES = 16
 SLAB = 64
-FIRST, EARLY, BETWEEN, LATE = 0, 30, 31, 46
+FIRST, EARLY, BETWEEN, LATE = 2, 28, 29, 48
 COPIES = 6 + 12 + 12 + 16 + 8 + 2 * (2 + 4 + 2 + 2) + 2
 TILES = 8
 EXTRA = 128
 
 
 def layer_kernel(
-    held_ref, swapped_ref, tokens_ref, logits_ref, routes_ref, wg_ref, wu_ref, wd_ref,
+    held_ref, swapped_ref, tokens_ref, logits_hbm, routes_hbm, wg_ref, wu_ref, wd_ref,
     mixed_ref, og_ref, ou_ref, od_ref, all_ref,
-    wg_v, wu_v, wd_v, tok_ref, tile_v, hall, relay, sel_v, wcol_v,
+    wg_v, wu_v, wd_v, logits_ref, routes_ref, tok_ref, tile_v, hall, relay, sel_v, wcol_v,
     hop0, got0, sum0, hop1, got1, sum1, last,
     local_sem, tile_sem, send_sem, recv_sem, swap_send, swap_recv,
 ):
@@ -92,7 +92,11 @@
         for k, (src, dst) in enumerate(((wg_ref, wg_v), (wu_ref, wu_v), (wd_ref, wd_v)))
     ]
     tok_load = pltpu.make_async_copy(tokens_ref, tok_ref.at[:, :, pl.ds(0, quarter)], local_sem.at[5])
-    for copy in [tok_load, *loads]:
+    route_loads = [
+        pltpu.make_async_copy(logits_hbm, logits_ref, local_sem.at[6]),
+        pltpu.make_async_copy(routes_hbm, routes_ref, local_sem.at[7]),
+    ]
+    for copy in [*route_loads, tok_load, *loads]:
         copy.start()
     greet(along_z + along_x + along_y + [sibling])
 
@@ -126,6 +130,8 @@
 
     swap_until(FIRST)
 
+    for copy in route_loads:
+        copy.wait()
     exp_count = held_ref.shape[0]
     top, here = logits_ref.shape[1:]
     lane_i = lax.broadcasted_iota(jnp.int32, (EXTRA, here), 0)
@@ -395,25 +401,33 @@
         sum1[s] = (sum0[s, away, at] + got1[s, 0, away] + got1[s, 1, away]).astype(jnp.bfloat16)
         finals.append(send(sum1.at[s], last.at[s], partner))
     swap_until(3 * PIECES)
+
+    flag = swapped_ref[lax.rem(lax.axis_index("exp"), swapped_ref.shape[0])]
+    settled = [0]
+
+    def settle(count):
+        while settled[0] < count:
+            n = settled[0]
+            dst, src = ((og_ref, wg_v), (ou_ref, wu_v), (od_ref, wd_v))[n // PIECES]
+            size = src.shape[0] // PIECES
+            start = n % PIECES * size
+            swaps[n].wait_recv()
+
+            @pl.loop(0, size // SLAB)
+            def _(i, dst=dst, src=src, start=start):
+                at = pl.ds(pl.multiple_of(start + i * SLAB, SLAB), SLAB)
+                trade = jnp.full((SLAB, src.shape[1]), flag, jnp.int32) == 1
+                dst[at, :] = jnp.where(trade, dst[at, :], src[at, :])
+
+            settled[0] += 1
+
+    settle(LATE - 2)
     for s in range(STEPS):
         at = spot_on[flow[s][1]]
         finals[s].wait_recv()
         total = sum0[s, z_lo, at] + got1[s, 0, z_lo] + got1[s, 1, z_lo] + last[s].astype(jnp.float32)
         mixed_ref[s] = total.astype(jnp.bfloat16)
-    flag = swapped_ref[lax.rem(lax.axis_index("exp"), swapped_ref.shape[0])]
-    n = 0
-    for dst, src in ((og_ref, wg_v), (ou_ref, wu_v), (od_ref, wd_v)):
-        size = src.shape[0] // PIECES
-        for k in range(PIECES):
-            swaps[n].wait_recv()
-
-            @pl.loop(0, size // SLAB)
-            def _(i, dst=dst, src=src, k=k, size=size):
-                at = pl.ds(pl.multiple_of(k * size + i * SLAB, SLAB), SLAB)
-                trade = jnp.full((SLAB, src.shape[1]), flag, jnp.int32) == 1
-                dst[at, :] = jnp.where(trade, dst[at, :], src[at, :])
-
-            n += 1
+    settle(3 * PIECES)
     for copy in send.copies + swaps:
         copy.wait_send()
 
@@ -437,12 +451,14 @@
             like(w_down),
             jax.ShapeDtypeStruct((steps, *plane, 4 * wide), dt),
         ),
-        in_specs=[smem, smem, pl.BlockSpec(memory_space=pltpu.HBM), vmem, vmem, hbm, hbm, hbm],
+        in_specs=[smem, smem, *[pl.BlockSpec(memory_space=pltpu.HBM)] * 3, hbm, hbm, hbm],
         out_specs=(vmem, vmem, vmem, vmem, hbm),
         scratch_shapes=[
             pltpu.VMEM(w_gate.shape, dt),
             pltpu.VMEM(w_up.shape, dt),
             pltpu.VMEM(w_down.shape, dt),
+            pltpu.VMEM(logits.shape, logits.dtype),
+            pltpu.VMEM(routes.shape, routes.dtype),
             pltpu.VMEM((steps, rows, wide), dt),
             pltpu.VMEM((2, 2, RING, rows, 4 * wide), dt),
             pltpu.VMEM((4, TILES, 4 * rows, part), dt),
@@ -456,7 +472,7 @@
             pltpu.VMEM((steps, 2, 2, rows, quarter), jnp.float32),
             pltpu.VMEM((steps, rows, quarter), dt),
             pltpu.VMEM((steps, rows, quarter), dt),
-            pltpu.SemaphoreType.DMA((6,)),
+            pltpu.SemaphoreType.DMA((8,)),
             pltpu.SemaphoreType.DMA((2,)),
             pltpu.SemaphoreType.DMA((COPIES,)),
             pltpu.SemaphoreType.DMA((COPIES,)),
@@ -503,6 +519,7 @@
 
 def per_device(tokens, logits, routes, held, swapped, w_gate, w_up, w_down):
     by_choice = (jnp.swapaxes(logits, 1, 2), jnp.swapaxes(routes, 1, 2))
+    tokens, *by_choice = (pltpu.with_memory_space_constraint(a, pltpu.HBM) for a in (tokens, *by_choice))
     mixed, *tiles = layer(held, swapped, tokens, *by_choice, w_gate[0], w_up[0], w_down[0])
     mixed, *tiles = store(mixed, *tiles)
     return (mixed, *(tile[None] for tile in tiles))

time: 275 us -> 273 us (level)
  no operation moved by 1% of the time
where the time goes in v5:
time: 273 us; the launch traced here: 272 us
  Pallas kernels  271 us (99%)
    pallas_call x1, Pallas kernels, layer(): pl.pallas_call(layer_kernel, out_shape=(jax.ShapeDtypeStruct((steps, rows...  266 us

profile of v5, /device:TPU:0, one launch (start us, length us, event | category | flops | bytes accessed | tf_op | source)
XLA Modules:
  0.0 272.5 jit_solution(12949667304598162295)
XLA Ops:
  0.6 0.0 copy-start
  0.6 0.6 copy-done
  1.3 0.0 copy-start.1
  1.3 0.7 copy-done.1
  1.9 266.2 %layer.1 = (bf16[2,32,1792]{2,1,0:T(8,128)(2,1)S(1)}, bf16[7168,256]{1,0:T(8,128)(2,1)S(1)}, bf16[7168,256]{1,0:T(8,128)(2,1)S(1)}, bf16[1024,1792]{1,0:T(8,128)(2,1)S(1)}, bf16[2,2,4,4,32,7680]{5,4,3,2,1,0:T(8,128)(2,1)}) custom-call(s32[32]{0:T(128)S(1)} %copy-done, s32[16]{0:T(128)S(1)} %copy-done.1, bf16[2,32,1792]{2,1,0:T(8,128)(2,1)} %tokens_ref.1, ...), custom_call_target="tpu_custom_call" | custom-call | tf_op jit(solution)/shard_map/layer/pallas_call | solution.py:445
  268.2 4.3 %store.1 = (bf16[2,32,1792]{2,1,0:T(8,128)(2,1)}, bf16[7168,256]{1,0:T(8,128)(2,1)}, bf16[7168,256]{1,0:T(8,128)(2,1)}, bf16[1024,1792]{1,0:T(8,128)(2,1)}) custom-call(bf16[2,32,1792]{2,1,0:T(8,128)(2,1)S(1)} %get-tuple-element.12.refs_0_, bf16[7168,256]{1,0:T(8,128)(2,1)S(1)} %get-tuple-element.13.refs_1_, ...), custom_call_target="tpu_custom_call" | custom-call | tf_op jit(solution)/shard_map/store/pallas_call | solution.py:509
Async XLA Ops:
  0.6 0.7 copy-start
  1.3 0.7 copy-start.1

commit v6 on v5

--- a/solution.py
+++ b/solution.py
@@ -71,9 +71,9 @@
 
 
 def layer_kernel(
-    held_ref, swapped_ref, tokens_ref, logits_hbm, routes_hbm, wg_ref, wu_ref, wd_ref,
+    held_hbm, swapped_hbm, tokens_ref, logits_hbm, routes_hbm, wg_ref, wu_ref, wd_ref,
     mixed_ref, og_ref, ou_ref, od_ref, all_ref,
-    wg_v, wu_v, wd_v, logits_ref, routes_ref, tok_ref, tile_v, hall, relay, sel_v, wcol_v,
+    wg_v, wu_v, wd_v, held_ref, swapped_ref, logits_ref, routes_ref, tok_ref, tile_v, hall, relay, sel_v, wcol_v,
     hop0, got0, sum0, hop1, got1, sum1, last,
     local_sem, tile_sem, send_sem, recv_sem, swap_send, swap_recv,
 ):
@@ -95,6 +95,8 @@
     route_loads = [
         pltpu.make_async_copy(logits_hbm, logits_ref, local_sem.at[6]),
         pltpu.make_async_copy(routes_hbm, routes_ref, local_sem.at[7]),
+        pltpu.make_async_copy(held_hbm, held_ref, local_sem.at[8]),
+        pltpu.make_async_copy(swapped_hbm, swapped_ref, local_sem.at[9]),
     ]
     for copy in [*route_loads, tok_load, *loads]:
         copy.start()
@@ -440,7 +442,6 @@
     plane = (2, RING, RING, rows)
     hbm = pl.BlockSpec(memory_space=pl.ANY)
     vmem = pl.BlockSpec(memory_space=pltpu.VMEM)
-    smem = pl.BlockSpec(memory_space=pltpu.SMEM)
     like = lambda a: jax.ShapeDtypeStruct(a.shape, a.dtype)
     return pl.pallas_call(
         layer_kernel,
@@ -451,12 +452,14 @@
             like(w_down),
             jax.ShapeDtypeStruct((steps, *plane, 4 * wide), dt),
         ),
-        in_specs=[smem, smem, *[pl.BlockSpec(memory_space=pltpu.HBM)] * 3, hbm, hbm, hbm],
+        in_specs=[*[pl.BlockSpec(memory_space=pltpu.HBM)] * 5, hbm, hbm, hbm],
         out_specs=(vmem, vmem, vmem, vmem, hbm),
         scratch_shapes=[
             pltpu.VMEM(w_gate.shape, dt),
             pltpu.VMEM(w_up.shape, dt),
             pltpu.VMEM(w_down.shape, dt),
+            pltpu.SMEM(held.shape, held.dtype),
+            pltpu.SMEM(swapped.shape, swapped.dtype),
             pltpu.VMEM(logits.shape, logits.dtype),
             pltpu.VMEM(routes.shape, routes.dtype),
             pltpu.VMEM((steps, rows, wide), dt),
@@ -472,7 +475,7 @@
             pltpu.VMEM((steps, 2, 2, rows, quarter), jnp.float32),
             pltpu.VMEM((steps, rows, quarter), dt),
             pltpu.VMEM((steps, rows, quarter), dt),
-            pltpu.SemaphoreType.DMA((8,)),
+            pltpu.SemaphoreType.DMA((10,)),
             pltpu.SemaphoreType.DMA((2,)),
             pltpu.SemaphoreType.DMA((COPIES,)),
             pltpu.SemaphoreType.DMA((COPIES,)),
@@ -519,7 +522,9 @@
 
 def per_device(tokens, logits, routes, held, swapped, w_gate, w_up, w_down):
     by_choice = (jnp.swapaxes(logits, 1, 2), jnp.swapaxes(routes, 1, 2))
-    tokens, *by_choice = (pltpu.with_memory_space_constraint(a, pltpu.HBM) for a in (tokens, *by_choice))
+    held, swapped, tokens, *by_choice = (
+        pltpu.with_memory_space_constraint(a, pltpu.HBM) for a in (held, swapped, tokens, *by_choice)
+    )
     mixed, *tiles = layer(held, swapped, tokens, *by_choice, w_gate[0], w_up[0], w_down[0])
     mixed, *tiles = store(mixed, *tiles)
     return (mixed, *(tile[None] for tile in tiles))

time: 273 us -> 271 us (level)
  no operation moved by 1% of the time
where the time goes in v6:
time: 271 us
  Pallas kernels  270 us (100%)
    pallas_call x1, Pallas kernels, layer(): pl.pallas_call(layer_kernel, out_shape=(jax.ShapeDtypeStruct((steps, rows...  266 us

profile of v6, /device:TPU:0, one launch (start us, length us, event | category | flops | bytes accessed | tf_op | source)
XLA Modules:
  0.0 270.7 jit_solution(17664839454002154127)
XLA Ops:
  0.6 265.8 %layer.1 = (bf16[2,32,1792]{2,1,0:T(8,128)(2,1)S(1)}, bf16[7168,256]{1,0:T(8,128)(2,1)S(1)}, bf16[7168,256]{1,0:T(8,128)(2,1)S(1)}, bf16[1024,1792]{1,0:T(8,128)(2,1)S(1)}, bf16[2,2,4,4,32,7680]{5,4,3,2,1,0:T(8,128)(2,1)}) custom-call(s32[32]{0:T(128)} %held_hbm.1, s32[16]{0:T(128)} %swapped_hbm.1, bf16[2,32,1792]{2,1,0:T(8,128)(2,1)} %tokens_ref.1, ...), custom_call_target="tpu_custom_call" | custom-call | tf_op jit(solution)/shard_map/layer/pallas_call | solution.py:446
  266.4 4.3 %store.1 = (bf16[2,32,1792]{2,1,0:T(8,128)(2,1)}, bf16[7168,256]{1,0:T(8,128)(2,1)}, bf16[7168,256]{1,0:T(8,128)(2,1)}, bf16[1024,1792]{1,0:T(8,128)(2,1)}) custom-call(bf16[2,32,1792]{2,1,0:T(8,128)(2,1)S(1)} %get-tuple-element.12.refs_0_, bf16[7168,256]{1,0:T(8,128)(2,1)S(1)} %get-tuple-element.13.refs_1_, ...), custom_call_target="tpu_custom_call" | custom-call | tf_op jit(solution)/shard_map/store/pallas_call | solution.py:512
